TPU v7x, 128 devices: a whole 4x4x4 slice. The times are simulated.
128 devices in a mesh: cam: 4 (over y), ex: 8 (over x_hi, z), ey: 4 (over x_lo, core).
Axes of the slice: x: 4 (x_hi: 2, x_lo: 2; x = x_hi * 2 + x_lo), y: 4, z: 4, core: 2. Of those that a mesh axis runs over, the one named last changes fastest.
Arguments:
- scalar: float32 [32, 8, 32, 8, 512], P('ex', None, 'ey', None, 'cam'), may hold values from -3 to 3
- velocity: float32 [3, 32, 8, 32, 8, 512], P(None, 'ex', None, 'ey', None, 'cam'), may hold values from -6 to 6
- lumped_mass: float32 [32, 8, 32, 8, 512], P('ex', None, 'ey', None, 'cam'), may hold values from 0.3 to 3
- pixel_weights: bfloat16 [8, 512, 128], replicated, may hold values from -0.25 to 0.25
- cut_element: int32 [8, 16384], P(None, ('cam', 'ex', 'ey')), may hold values from 0 to 511
- pixel_block: int32 [8, 16384], P(None, ('cam', 'ex', 'ey')), may hold values from 0 to 1024, as said below
Outputs:
- advected: float32 [32, 8, 32, 8, 512], P('ex', None, 'ey', None, 'cam')
- images: float32 [8, 32768, 128], P('cam', ('ex', 'ey'))
Inputs may be any that keep to these rules, and one draw needn't show every extreme that they name: `pixel_block`: A value of 1024 marks an empty slot; in each device's 128 slots of one camera the filled ones come first. `cut_element`: A local element number of the owning device, with the radial index fastest, then the azimuthal, then the axial.
All inputs are finite; a program needn't handle non-finite values.
Results may differ from a plain program's by a relative error of at most 0.0028.
Values may be sent and summed in bfloat16 or wider, within the bound.
A program may use at most 64 MiB of HBM per device.

v0:
```python
import jax
import jax.numpy as jnp
import numpy as np
from jax import lax
from jax.sharding import PartitionSpec as P

NBLK = 1024


time_step = 0.01


def padded(shard, sides, width, wrap):
    for axis, dim in sides:
        count, length = (lax.axis_size(axis), shard.shape[dim])
        up = [(i, (i + 1) % count) for i in range(count if wrap else count - 1)]
        down = [(j, i) for i, j in up]
        last = lax.slice_in_dim(shard, length - width, length, axis=dim)
        initial = lax.slice_in_dim(shard, 0, width, axis=dim)
        before = lax.ppermute(last, axis, up)
        after = lax.ppermute(initial, axis, down)
        shard = jnp.concatenate([before, shard, after], axis=dim)
    return shard


def legendre_seven(points):
    previous = points * 0.0 + 1.0
    current = points * 1.0
    for order in range(1, 7):
        following = ((2 * order + 1) * points * current - order * previous) / (order + 1)
        previous = current
        current = following
    return current


def gll_derivative():
    degree = 7
    gll_nodes = np.array(
        [
            -1.0,
            -0.8717401485096066,
            -0.5917001814331423,
            -0.2092992179024789,
            0.2092992179024789,
            0.5917001814331423,
            0.8717401485096066,
            1.0,
        ]
    )
    values = legendre_seven(gll_nodes)
    derivative = np.zeros((degree + 1, degree + 1))
    for target in range(degree + 1):
        for source in range(degree + 1):
            if target != source:
                derivative[target, source] = values[target] / (
                    values[source] * (gll_nodes[target] - gll_nodes[source])
                )
    derivative[0, 0] = -degree * (degree + 1) / 4.0
    derivative[degree, degree] = degree * (degree + 1) / 4.0
    return derivative


def pair_sum(extended, dim):
    length = extended.shape[dim] - 2
    middle = lax.slice_in_dim(extended, 1, length + 1, 1, dim)
    following = lax.slice_in_dim(extended, 2, length + 2, 1, dim)
    preceding = lax.slice_in_dim(extended, 0, length, 1, dim)
    shape = [1] * extended.ndim
    shape[dim] = length
    node = (jnp.arange(length, dtype=jnp.int32) % 8).reshape(shape)
    is_last = (node == 7).astype(jnp.float32)
    is_first = (node == 0).astype(jnp.float32)
    return middle + is_last * following + is_first * preceding


def assemble(stack):
    extended = padded(stack, (("ex", 1),), 1, True)
    summed = pair_sum(extended, 1)
    extended = padded(summed, (("ey", 2),), 1, True)
    summed = pair_sum(extended, 2)
    extended = padded(summed, (("cam", 3),), 1, False)
    return pair_sum(extended, 3)


def convect(field, velocity, derivative, radial_table):
    along_axial = jnp.einsum("pi,aibjz->apbjz", derivative, field, precision=lax.Precision.HIGHEST)
    along_azimuth = jnp.einsum(
        "qj,aibjz->aibqz", derivative, field, precision=lax.Precision.HIGHEST
    )
    along_radius = jnp.dot(field, radial_table, precision=lax.Precision.HIGHEST)
    return velocity[0] * along_axial + velocity[1] * along_azimuth + velocity[2] * along_radius


def per_device(scalar, velocity, lumped_mass, pixel_weights, cut_element, pixel_block):
    shape = scalar.shape
    depth = shape[4]
    derivative = jnp.asarray(gll_derivative(), jnp.float32)
    radial_table = jnp.kron(jnp.eye(depth // 8, dtype=jnp.float32), derivative.T)
    flat = (shape[0] * 8, shape[2] * 8, depth)
    first_stack = jnp.stack(
        [
            (lumped_mass * convect(scalar, velocity, derivative, radial_table)).reshape(flat),
            lumped_mass.reshape(flat),
        ]
    )
    first_sums = assemble(first_stack)
    assembled_mass = first_sums[1]
    rate_first = (first_sums[0] / assembled_mass).reshape(shape)
    first = scalar - time_step * rate_first
    second_stack = (lumped_mass * convect(first, velocity, derivative, radial_table)).reshape(
        (1,) + flat
    )
    rate_second = (assemble(second_stack)[0] / assembled_mass).reshape(shape)
    second = first - time_step * rate_second
    advected = 0.5 * (scalar + second)
    element_count = shape[0] * shape[2] * (depth // 8)
    elements = (
        advected.astype(jnp.bfloat16)
        .reshape(shape[0], 8, shape[2], 8, depth // 8, 8)
        .transpose(0, 2, 4, 1, 3, 5)
        .reshape(element_count, 512)
    )
    picked = jnp.take(elements, cut_element, axis=0)
    block_ids = jnp.arange(NBLK, dtype=jnp.int32)
    values = jnp.einsum("csp,cpx->csx", picked, pixel_weights, preferred_element_type=jnp.float32)
    onehot = (pixel_block[:, None, :] == block_ids[None, :, None]).astype(jnp.float32)
    images = lax.psum_scatter(
        jnp.einsum("cbs,csx->cbx", onehot, values, precision=lax.Precision.HIGHEST),
        "cam",
        scatter_dimension=0,
        tiled=True,
    )
    return (advected, images)


def solution(mesh):
    placed = (
        P("ex", None, "ey", None, "cam"),
        P(None, "ex", None, "ey", None, "cam"),
        P("ex", None, "ey", None, "cam"),
        P(),
        P(None, ("cam", "ex", "ey")),
        P(None, ("cam", "ex", "ey")),
    )
    return jax.shard_map(
        per_device,
        mesh=mesh,
        in_specs=placed,
        out_specs=(P("ex", None, "ey", None, "cam"), P("cam", ("ex", "ey"), None)),
        check_vma=False,
    )
```

profile of v0, /device:TPU:1, one launch (start us, length us, event | category | flops | bytes accessed | tf_op | source)
XLA Modules:
  0.0 191.1 jit_solution(16086688268746747414)
XLA Ops:
  7.2 3.8 %fusion.53 = (f32[1,4,8,8,8,128]{5,4,3,2,1,0:T(8,128)}, f32[1,4,8,8,8,128]{5,4,3,2,1,0:T(8,128)}, f32[1,4,8,8,8,128]{5,4,3,2,1,0:T(8,128)}) fusion(f32[3,4,8,8,8,128]{5,4,3,2,1,0:T(8,128)} %param.8), kind=kLoop, calls=%fused_computation.99 | loop fusion | bytes 6291456 | tf_op jit(solution)/shard_map/slice | solution.py:91
  13.8 3.1 %fusion.20 = f32[4,8,8,8,128]{4,1,3,2,0:T(8,128)S(1)} fusion(f32[8,8,1,1,1]{1,0,4,3,2:T(8,128)S(1)} %copy-done.13, f32[8,4,8,8,128]{4,0,3,2,1:T(8,128)S(1)} %fusion.59, f32[1,4,8,8,8,128]{5,4,3,2,1,0:T(8,128)S(1)} %copy-done.11, f32[1,4,8,8,8,128]{5,4,3,2,1,0:T(8,128)S(1)} %copy-done.9, f32[4,8,8,8,128]{4,3,2,1,0:T(8,128)S(1)} %copy-done.1), kind=kOutput, calls=%fused_computation.39 | convolution fusion | flops 25952256 | bytes 5243136 | tf_op jit(solution)/shard_map/pi,aibjz->apbjz/dot_general | solution.py:86
  16.9 2.4 %fusion.21 = f32[4,8,8,8,128]{4,1,3,2,0:T(8,128)S(1)} fusion(f32[4,8,8,8,128]{4,1,3,2,0:T(8,128)S(1)} %fusion.20, f32[1,4,8,8,8,128]{5,4,3,2,1,0:T(8,128)S(1)} %copy-done.7, f32[4,8,8,8,128]{4,3,2,1,0:T(8,128)S(1)} %copy-done.3, f32[4,8,8,8,128]{4,3,2,1,0:T(8,128)S(1)} %copy-done.1, f32[128,128,1,1,1]{1,0,2,3,4:T(8,128)S(1)} %reshape.95), kind=kOutput, calls=%fused_computation.40 | convolution fusion | flops 403439616 | bytes 5308416 | tf_op jit(solution)/shard_map/dot_general | solution.py:90
  19.6 2.5 %collective-permute-start.1 = (f32[2,1,64,128]{3,2,1,0:T(8,128)S(1)}, f32[2,1,64,128]{3,2,1,0:T(8,128)S(1)}, u32[]{:S(2)}, u32[]{:S(2)}) collective-permute-start(f32[2,1,64,128]{3,2,1,0:T(8,128)S(1)} %get-tuple-element.12), channel_id=1, source_target_pairs={{0,4},{4,8},{8,12},{12,16},{16,20},{20,24},{24,28},{28,0},{1,5},{5... | collective-permute-start | bytes 196616 | tf_op jit(solution)/shard_map/ppermute | solution.py:20
  22.1 4.7 %collective-permute-start = (f32[2,1,64,128]{3,2,1,0:T(8,128)S(1)}, f32[2,1,64,128]{3,2,1,0:T(8,128)S(1)}, u32[]{:S(2)}, u32[]{:S(2)}) collective-permute-start(f32[2,1,64,128]{3,2,1,0:T(8,128)S(1)} %get-tuple-element.11), channel_id=1, source_target_pairs={{4,0},{8,4},{12,8},{16,12},{20,16},{24,20},{28,24},{0,28},{5,1},{9... | collective-permute-start | bytes 196616 | tf_op jit(solution)/shard_map/ppermute | solution.py:21
  26.8 1.6 collective-permute-done.1
  28.8 1.8 collective-permute-start.3
  31.7 2.3 %collective-permute-done.2 = f32[2,32,1,128]{3,2,1,0:T(1,128)S(1)} collective-permute-done((f32[2,32,1,128]{3,2,1,0:T(1,128)S(1)}, f32[2,32,1,128]{3,2,1,0:T(1,128)S(1)}, u32[]{:S(2)}, u32[]{:S(2)}) %collective-permute-start.2) | collective-permute-done | bytes 32800 | tf_op jit(solution)/shard_map/ppermute | solution.py:21
  34.8 2.9 %fusion.54 = (f32[2,32,64,1]{3,2,1,0:T(8,128)}, f32[2,32,64,1]{3,2,1,0:T(8,128)}) fusion(f32[2,32,64,128]{3,2,1,0:T(8,128)S(1)} %fusion.8), kind=kLoop, calls=%fused_computation.100 | loop fusion | bytes 65536 | tf_op jit(solution)/shard_map/slice | solution.py:19
  37.7 2.3 %copy.46 = f32[2,32,64,1]{2,1,3,0:T(8,128)S(1)} copy(f32[2,32,64,1]{3,2,1,0:T(8,128)} %get-tuple-element.8) | data formatting | bytes 32768 | tf_op jit(solution)/shard_map/slice | solution.py:18
  40.0 3.4 %collective-permute-start.5 = (f32[2,32,64,1]{2,1,3,0:T(8,128)S(1)}, f32[2,32,64,1]{2,1,3,0:T(8,128)S(1)}, u32[]{:S(2)}, u32[]{:S(2)}) collective-permute-start(f32[2,32,64,1]{2,1,3,0:T(8,128)S(1)} %copy.46), channel_id=1, source_target_pairs={{0,32},{32,64},{64,96},{1,33},{33,65},{65,97},{2,34},{34,66},{66,9... | collective-permute-start | bytes 49160 | tf_op jit(solution)/shard_map/ppermute | solution.py:20
  43.4 2.3 %copy.44 = f32[2,32,64,1]{2,1,3,0:T(8,128)S(1)} copy(f32[2,32,64,1]{3,2,1,0:T(8,128)} %get-tuple-element.7) | data formatting | bytes 32768 | tf_op jit(solution)/shard_map/slice | solution.py:19
  47.0 2.1 %copy.47 = f32[2,32,64,1]{3,2,1,0:T(8,128)} copy(f32[2,32,64,1]{2,1,3,0:T(8,128)S(1)} %collective-permute-done.5) | data formatting | bytes 32768 | tf_op jit(solution)/shard_map/ppermute | solution.py:20
  50.3 2.0 %copy.45 = f32[2,32,64,1]{3,2,1,0:T(8,128)} copy(f32[2,32,64,1]{2,1,3,0:T(8,128)S(1)} %collective-permute-done.4) | data formatting | bytes 32768 | tf_op jit(solution)/shard_map/ppermute | solution.py:21
  52.3 3.9 %fusion.4 = f32[2,32,64,128]{3,2,1,0:T(8,128)S(1)} fusion(f32[2,32,64,128]{3,2,1,0:T(8,128)S(1)} %fusion.8, f32[2,32,64,1]{3,2,1,0:T(8,128)} %copy.47, f32[2,32,64,1]{3,2,1,0:T(8,128)} %copy.45, f32[128]{0:T(128)S(1)} %get-tuple-element.23, f32[128]{0:T(128)S(1)} %get-tuple-element.24), kind=kLoop, calls=%fused_computation.12 | loop fusion | flops 3145728 | bytes 4228096 | tf_op jit(solution)/shard_map/add | solution.py:73
  56.4 1.8 copy-done.2
  59.8 3.2 %fusion.16 = f32[4,8,8,8,128]{4,1,3,2,0:T(8,128)S(1)} fusion(f32[8,8,1,1,1]{1,0,4,3,2:T(8,128)S(1)} %copy-done.13, f32[4,8,8,128,8]{3,4,2,1,0:T(8,128)S(1)} %fusion.60, f32[1,4,8,8,8,128]{5,4,3,2,1,0:T(8,128)S(1)} %copy-done.12, f32[1,4,8,8,8,128]{5,4,3,2,1,0:T(8,128)S(1)} %copy-done.10, f32[4,8,8,8,128]{4,3,2,1,0:T(8,128)S(1)} %sub.6), kind=kOutput, calls=%fused_computation.33 | convolution fusion | flops 25952256 | bytes 5243136 | tf_op jit(solution)/shard_map/pi,aibjz->apbjz/dot_general | solution.py:86
  63.0 2.4 %fusion.22 = f32[4,8,8,8,128]{4,1,3,2,0:T(8,128)S(1)} fusion(f32[4,8,8,8,128]{4,1,3,2,0:T(8,128)S(1)} %fusion.16, f32[1,4,8,8,8,128]{5,4,3,2,1,0:T(8,128)S(1)} %copy-done.8, f32[4,8,8,8,128]{4,3,2,1,0:T(8,128)S(1)} %sub.6, f32[4,8,8,8,128]{4,3,2,1,0:T(8,128)S(1)} %copy-done.4, f32[128,128,1,1,1]{1,0,2,3,4:T(8,128)S(1)} %reshape.95), kind=kOutput, calls=%fused_computation.41 | convolution fusion | flops 403439616 | bytes 5308416 | tf_op jit(solution)/shard_map/dot_general | solution.py:90
  65.8 6.6 %collective-permute-start.6 = (f32[1,1,64,128]{3,2,1,0:T(8,128)S(1)}, f32[1,1,64,128]{3,2,1,0:T(8,128)S(1)}, u32[]{:S(2)}, u32[]{:S(2)}) collective-permute-start(f32[1,1,64,128]{3,2,1,0:T(8,128)S(1)} %get-tuple-element.17), channel_id=1, source_target_pairs={{4,0},{8,4},{12,8},{16,12},{20,16},{24,20},{28,24},{0,28},{5,1},{9... | collective-permute-start | bytes 98312 | tf_op jit(solution)/shard_map/ppermute | solution.py:21
  76.0 2.3 %collective-permute-done.8 = f32[1,32,1,128]{3,2,1,0:T(1,128)S(1)} collective-permute-done((f32[1,32,1,128]{3,2,1,0:T(1,128)S(1)}, f32[1,32,1,128]{3,2,1,0:T(1,128)S(1)}, u32[]{:S(2)}, u32[]{:S(2)}) %collective-permute-start.8) | collective-permute-done | bytes 16416 | tf_op jit(solution)/shard_map/ppermute | solution.py:21
  78.7 1.7 fusion.56
  80.4 1.6 copy.55
  82.0 3.2 %collective-permute-start.11 = (f32[1,32,64,1]{2,1,3,0:T(8,128)S(1)}, f32[1,32,64,1]{2,1,3,0:T(8,128)S(1)}, u32[]{:S(2)}, u32[]{:S(2)}) collective-permute-start(f32[1,32,64,1]{2,1,3,0:T(8,128)S(1)} %copy.55), channel_id=1, source_target_pairs={{0,32},{32,64},{64,96},{1,33},{33,65},{65,97},{2,34},{34,66},{66,9... | collective-permute-start | bytes 24584 | tf_op jit(solution)/shard_map/ppermute | solution.py:20
  85.2 1.6 copy.53
  89.5 1.8 collective-permute-done.10
  92.7 3.8 %fusion.26 = f32[1,32,64,128]{3,2,1,0:T(8,128)S(1)} fusion(f32[1,32,64,128]{3,2,1,0:T(8,128)} %copy-done.5, f32[1,32,64,1]{3,2,1,0:T(8,128)} %copy.56, f32[1,32,64,1]{3,2,1,0:T(8,128)} %copy.54, f32[2,32,64,128]{3,2,1,0:T(8,128)} %copy-done.6, f32[128]{0:T(128)S(1)} %get-tuple-element.23, f32[128]{0:T(128)S(1)} %get-tuple-element.24), kind=kLoop, calls=%fused_computation.46 | loop fusion | flops 2097152 | bytes 3163136 | tf_op jit(solution)/shard_map/mul | solution.py:114
  98.0 11.9 %reshape.82 = bf16[4,8,8,8,16,8]{5,4,3,2,1,0:T(8,128)(2,1)} reshape(bf16[4,8,8,8,128]{4,3,2,1,0:T(8,128)(2,1)} %get-tuple-element.2) | data formatting | bytes 1048576 | tf_op jit(solution)/shard_map/reshape | solution.py:119
  109.9 10.5 %copy.57 = bf16[4,8,16,8,8,8]{2,1,0,5,4,3:T(8,128)(2,1)} copy(bf16[4,8,16,8,8,8]{5,2,4,1,3,0:T(8,128)(2,1)} %bitcast.79) | data formatting | bytes 1048576 | tf_op jit(solution)/shard_map/transpose | solution.py:120
  120.4 7.8 %reshape.83 = bf16[512,512]{0,1:T(8,128)(2,1)S(1)} reshape(bf16[4,8,16,8,8,8]{2,1,0,5,4,3:T(8,128)(2,1)} %copy.57) | data formatting | bytes 1048576 | tf_op jit(solution)/shard_map/reshape | solution.py:121
  128.4 4.0 %gather_fusion = bf16[1024,512]{1,0:T(8,128)(2,1)S(1)} fusion(bf16[512,512]{1,0:T(8,128)(2,1)S(1)} %copy.58, s32[1024]{0:T(1024)S(1)} %bitcast_clamp_fusion), kind=kCustom, calls=%fused_computation | custom fusion | bytes 2101248 | tf_op jit(solution)/shard_map/jit(_take)/gather | solution.py:123
  133.0 3.5 %fusion = f32[8,1024,128]{2,1,0:T(8,128)} fusion(f32[8,128,128]{2,1,0:T(8,128)S(1)} %fusion.38, s32[8,128]{1,0:T(8,128)S(1)} %copy-done.16), kind=kOutput, calls=%fused_computation.2 | convolution fusion | flops 1611661312 | bytes 4722688 | tf_op jit(solution)/shard_map/cbs,csx->cbx/dot_general | solution.py:128
  136.5 47.8 %reduce-scatter.2.cloned.1.call-done = f32[2,1024,128]{2,1,0:T(8,128)} async-done(((f32[8,1024,128]{2,1,0:T(8,128)}), f32[2,1024,128]{2,1,0:T(8,128)}) %reduce-scatter.2.cloned.1.call-update) | async-done | bytes 1048592 | tf_op jit(solution)/shard_map/reduce_scatter | solution.py:127
  (76 shorter events, 20.3 us)
Async XLA Ops:
  7.2 125.2 %copy-start = (bf16[8,512,128]{2,1,0:T(8,128)(2,1)S(1)}, bf16[8,512,128]{2,1,0:T(8,128)(2,1)}, u32[]{:S(2)}) copy-start(bf16[8,512,128]{2,1,0:T(8,128)(2,1)} %param.10) | copy-start | bytes 3145732
  7.2 177.1 %reduce-scatter.2.cloned.1.call-start = ((), (), s32[]{:S(2)}) async-start(), calls=%async_computation.1 | async-start | bytes 5242880 | tf_op jit(solution)/shard_map/reduce_scatter | solution.py:127
  7.2 3.8 %copy-start.15 = (f32[8,8]{1,0:T(8,128)S(1)}, f32[8,8]{1,0:T(8,128)}, u32[]{:S(2)}) copy-start(f32[8,8]{1,0:T(8,128)} %constant.74) | copy-start | bytes 772
  11.0 1.2 copy-start.1
  11.0 1.2 copy-start.13
  12.2 1.2 copy-start.9
  12.2 1.5 copy-start.11
  13.8 3.1 %copy-start.3 = (f32[4,8,8,8,128]{4,3,2,1,0:T(8,128)S(1)}, f32[4,8,8,8,128]{4,3,2,1,0:T(8,128)}, u32[]{:S(2)}) copy-start(f32[4,8,8,8,128]{4,3,2,1,0:T(8,128)} %param.9) | copy-start | bytes 3145732
  13.8 3.1 %copy-start.7 = (f32[1,4,8,8,8,128]{5,4,3,2,1,0:T(8,128)S(1)}, f32[1,4,8,8,8,128]{5,4,3,2,1,0:T(8,128)}, u32[]{:S(2)}) copy-start(f32[1,4,8,8,8,128]{5,4,3,2,1,0:T(8,128)} %get-tuple-element.4) | copy-start | bytes 3145732
  19.6 8.8 %collective-permute-start.1 = (f32[2,1,64,128]{3,2,1,0:T(8,128)S(1)}, f32[2,1,64,128]{3,2,1,0:T(8,128)S(1)}, u32[]{:S(2)}, u32[]{:S(2)}) collective-permute-start(f32[2,1,64,128]{3,2,1,0:T(8,128)S(1)} %get-tuple-element.12), channel_id=1, source_target_pairs={{0,4},{4,8},{8,12},{12,16},{16,20},{20,24},{24,28},{28,0},{1,5},{5... | collective-permute-start | bytes 196616 | tf_op jit(solution)/shard_map/ppermute | solution.py:20
  22.1 6.2 %collective-permute-start = (f32[2,1,64,128]{3,2,1,0:T(8,128)S(1)}, f32[2,1,64,128]{3,2,1,0:T(8,128)S(1)}, u32[]{:S(2)}, u32[]{:S(2)}) collective-permute-start(f32[2,1,64,128]{3,2,1,0:T(8,128)S(1)} %get-tuple-element.11), channel_id=1, source_target_pairs={{4,0},{8,4},{12,8},{16,12},{20,16},{24,20},{28,24},{0,28},{5,1},{9... | collective-permute-start | bytes 196616 | tf_op jit(solution)/shard_map/ppermute | solution.py:21
  28.8 2.9 %collective-permute-start.3 = (f32[2,32,1,128]{3,2,1,0:T(1,128)S(1)}, f32[2,32,1,128]{3,2,1,0:T(1,128)S(1)}, u32[]{:S(2)}, u32[]{:S(2)}) collective-permute-start(f32[2,32,1,128]{3,2,1,0:T(1,128)S(1)} %get-tuple-element.10), channel_id=1, source_target_pairs={{0,1},{1,2},{2,3},{3,0},{4,5},{5,6},{6,7},{7,4},{8,9},{9,10},{10,1... | collective-permute-start | bytes 98312 | tf_op jit(solution)/shard_map/ppermute | solution.py:20
  30.7 3.3 %collective-permute-start.2 = (f32[2,32,1,128]{3,2,1,0:T(1,128)S(1)}, f32[2,32,1,128]{3,2,1,0:T(1,128)S(1)}, u32[]{:S(2)}, u32[]{:S(2)}) collective-permute-start(f32[2,32,1,128]{3,2,1,0:T(1,128)S(1)} %get-tuple-element.9), channel_id=1, source_target_pairs={{1,0},{2,1},{3,2},{0,3},{5,4},{6,5},{7,6},{4,7},{9,8},{10,9},{11,1... | collective-permute-start | bytes 98312 | tf_op jit(solution)/shard_map/ppermute | solution.py:21
  40.0 7.0 %collective-permute-start.5 = (f32[2,32,64,1]{2,1,3,0:T(8,128)S(1)}, f32[2,32,64,1]{2,1,3,0:T(8,128)S(1)}, u32[]{:S(2)}, u32[]{:S(2)}) collective-permute-start(f32[2,32,64,1]{2,1,3,0:T(8,128)S(1)} %copy.46), channel_id=1, source_target_pairs={{0,32},{32,64},{64,96},{1,33},{33,65},{65,97},{2,34},{34,66},{66,9... | collective-permute-start | bytes 49160 | tf_op jit(solution)/shard_map/ppermute | solution.py:20
  45.6 4.7 %collective-permute-start.4 = (f32[2,32,64,1]{2,1,3,0:T(8,128)S(1)}, f32[2,32,64,1]{2,1,3,0:T(8,128)S(1)}, u32[]{:S(2)}, u32[]{:S(2)}) collective-permute-start(f32[2,32,64,1]{2,1,3,0:T(8,128)S(1)} %copy.44), channel_id=1, source_target_pairs={{32,0},{64,32},{96,64},{33,1},{65,33},{97,65},{34,2},{66,34},{98,6... | collective-permute-start | bytes 49160 | tf_op jit(solution)/shard_map/ppermute | solution.py:21
  56.2 2.1 %copy-start.6 = (f32[2,32,64,128]{3,2,1,0:T(8,128)}, f32[2,32,64,128]{3,2,1,0:T(8,128)S(1)}, u32[]{:S(2)}) copy-start(f32[2,32,64,128]{3,2,1,0:T(8,128)S(1)} %fusion.4) | copy-start | bytes 6291460
  56.2 2.0 %copy-start.2 = (f32[4,8,8,8,128]{4,3,2,1,0:T(8,128)S(1)}, f32[4,8,8,8,128]{4,3,2,1,0:T(8,128)}, u32[]{:S(2)}) copy-start(f32[4,8,8,8,128]{4,3,2,1,0:T(8,128)} %param.7) | copy-start | bytes 3145732
  58.2 1.2 copy-start.10
  58.2 1.5 copy-start.12
  59.8 3.2 %copy-start.4 = (f32[4,8,8,8,128]{4,3,2,1,0:T(8,128)S(1)}, f32[4,8,8,8,128]{4,3,2,1,0:T(8,128)}, u32[]{:S(2)}) copy-start(f32[4,8,8,8,128]{4,3,2,1,0:T(8,128)} %param.9) | copy-start | bytes 3145732
  59.8 3.3 %copy-start.8 = (f32[1,4,8,8,8,128]{5,4,3,2,1,0:T(8,128)S(1)}, f32[1,4,8,8,8,128]{5,4,3,2,1,0:T(8,128)}, u32[]{:S(2)}) copy-start(f32[1,4,8,8,8,128]{5,4,3,2,1,0:T(8,128)} %get-tuple-element.4) | copy-start | bytes 3145732
  65.5 10.0 %copy-start.14 = (s32[8,128]{1,0:T(8,128)S(1)}, s32[8,128]{1,0:T(8,128)}, u32[]{:S(2)}) copy-start(s32[8,128]{1,0:T(8,128)} %param.11) | copy-start | bytes 12292
  65.7 7.9 %collective-permute-start.7 = (f32[1,1,64,128]{3,2,1,0:T(8,128)S(1)}, f32[1,1,64,128]{3,2,1,0:T(8,128)S(1)}, u32[]{:S(2)}, u32[]{:S(2)}) collective-permute-start(f32[1,1,64,128]{3,2,1,0:T(8,128)S(1)} %get-tuple-element.18), channel_id=1, source_target_pairs={{0,4},{4,8},{8,12},{12,16},{16,20},{20,24},{24,28},{28,0},{1,5},{5... | collective-permute-start | bytes 98312 | tf_op jit(solution)/shard_map/ppermute | solution.py:20
  65.8 7.8 %collective-permute-start.6 = (f32[1,1,64,128]{3,2,1,0:T(8,128)S(1)}, f32[1,1,64,128]{3,2,1,0:T(8,128)S(1)}, u32[]{:S(2)}, u32[]{:S(2)}) collective-permute-start(f32[1,1,64,128]{3,2,1,0:T(8,128)S(1)} %get-tuple-element.17), channel_id=1, source_target_pairs={{4,0},{8,4},{12,8},{16,12},{20,16},{24,20},{28,24},{0,28},{5,1},{9... | collective-permute-start | bytes 98312 | tf_op jit(solution)/shard_map/ppermute | solution.py:21
  73.9 2.2 %collective-permute-start.9 = (f32[1,32,1,128]{3,2,1,0:T(1,128)S(1)}, f32[1,32,1,128]{3,2,1,0:T(1,128)S(1)}, u32[]{:S(2)}, u32[]{:S(2)}) collective-permute-start(f32[1,32,1,128]{3,2,1,0:T(1,128)S(1)} %get-tuple-element.16), channel_id=1, source_target_pairs={{0,1},{1,2},{2,3},{3,0},{4,5},{5,6},{6,7},{7,4},{8,9},{9,10},{10,1... | collective-permute-start | bytes 49160 | tf_op jit(solution)/shard_map/ppermute | solution.py:20
  75.2 3.2 %collective-permute-start.8 = (f32[1,32,1,128]{3,2,1,0:T(1,128)S(1)}, f32[1,32,1,128]{3,2,1,0:T(1,128)S(1)}, u32[]{:S(2)}, u32[]{:S(2)}) collective-permute-start(f32[1,32,1,128]{3,2,1,0:T(1,128)S(1)} %get-tuple-element.15), channel_id=1, source_target_pairs={{1,0},{2,1},{3,2},{0,3},{5,4},{6,5},{7,6},{4,7},{9,8},{10,9},{11,1... | collective-permute-start | bytes 49160 | tf_op jit(solution)/shard_map/ppermute | solution.py:21
  78.7 1.7 copy-start.5
  82.0 6.1 %collective-permute-start.11 = (f32[1,32,64,1]{2,1,3,0:T(8,128)S(1)}, f32[1,32,64,1]{2,1,3,0:T(8,128)S(1)}, u32[]{:S(2)}, u32[]{:S(2)}) collective-permute-start(f32[1,32,64,1]{2,1,3,0:T(8,128)S(1)} %copy.55), channel_id=1, source_target_pairs={{0,32},{32,64},{64,96},{1,33},{33,65},{65,97},{2,34},{34,66},{66,9... | collective-permute-start | bytes 24584 | tf_op jit(solution)/shard_map/ppermute | solution.py:20
  86.8 4.5 %collective-permute-start.10 = (f32[1,32,64,1]{2,1,3,0:T(8,128)S(1)}, f32[1,32,64,1]{2,1,3,0:T(8,128)S(1)}, u32[]{:S(2)}, u32[]{:S(2)}) collective-permute-start(f32[1,32,64,1]{2,1,3,0:T(8,128)S(1)} %copy.53), channel_id=1, source_target_pairs={{32,0},{64,32},{96,64},{33,1},{65,33},{97,65},{34,2},{66,34},{98,6... | collective-permute-start | bytes 24584 | tf_op jit(solution)/shard_map/ppermute | solution.py:21
  132.3 0.7 copy-start.16
Sparse Core Ops, SparseCore 0:
  136.6 47.6 reduce-scatter.1
where the time goes:
time: 192 us; the launch traced here: 191 us
  local copies, waits for them, and re-layouts  61.8 us (32%)
  waiting for transfers between devices  59.8 us (31%)
  starting transfers between devices  26.6 us (14%)
  matrix products  17.1 us (9%)
  between operations  14.4 us (8%)
  other arithmetic  11.5 us (6%)
    reduce_scatter x1, waiting for transfers between devices, per_device(): lax.psum_scatter(jnp.einsum('cbs,csx->cbx', onehot, values, precision=lax...  47.8 us
    reshape x3, local copies, waits for them, and re-layouts, per_device(): elements = advected.astype(jnp.bfloat16).reshape(shape[0], 8, shape[2], 8...  19.9 us
    ppermute x6, starting transfers between devices, padded(): after = lax.ppermute(initial, axis, down)  14.2 us
    ppermute x6, starting transfers between devices, padded(): before = lax.ppermute(last, axis, up)  12.3 us
    transpose x1, local copies, waits for them, and re-layouts, per_device(): elements = advected.astype(jnp.bfloat16).reshape(shape[0], 8, shape[2], 8...  10.5 us
    slice x7, local copies, waits for them, and re-layouts, padded(): initial = lax.slice_in_dim(shard, 0, width, axis=dim)  8.53 us
    ppermute x6, waiting for transfers between devices, padded(): after = lax.ppermute(initial, axis, down)  7.68 us
    dot_general x2, matrix products, convect(): jnp.einsum('pi,aibjz->apbjz', derivative, field, precision=lax.Precision....  6.33 us
  transfers between devices with their start and end apart: 13, of which 9 were waited for; matrix products, arithmetic and copies ran while one was open for 4% of the time, Pallas kernels for 0%

commit v1 on v0

v1 whole, which is shorter than its diff:
```python
import functools

import jax
import jax.numpy as jnp
import ml_dtypes
import numpy as np
from jax import lax
from jax.experimental import pallas as pl
from jax.experimental.pallas import tpu as pltpu
from jax.sharding import PartitionSpec as P

NBLK = 1024
STEP = 0.01
F32 = jnp.float32
BF16 = jnp.bfloat16


def legendre_seven(points):
    previous = points * 0.0 + 1.0
    current = points * 1.0
    for order in range(1, 7):
        following = ((2 * order + 1) * points * current - order * previous) / (order + 1)
        previous = current
        current = following
    return current


def gll_derivative():
    degree = 7
    gll_nodes = np.array(
        [
            -1.0,
            -0.8717401485096066,
            -0.5917001814331423,
            -0.2092992179024789,
            0.2092992179024789,
            0.5917001814331423,
            0.8717401485096066,
            1.0,
        ]
    )
    values = legendre_seven(gll_nodes)
    derivative = np.zeros((degree + 1, degree + 1))
    for target in range(degree + 1):
        for source in range(degree + 1):
            if target != source:
                derivative[target, source] = values[target] / (
                    values[source] * (gll_nodes[target] - gll_nodes[source])
                )
    derivative[0, 0] = -degree * (degree + 1) / 4.0
    derivative[degree, degree] = degree * (degree + 1) / 4.0
    return derivative


DERIV = gll_derivative()


def radial_matrix():
    table = np.kron(np.eye(16), DERIV.T).astype(np.float32)
    high = table.astype(ml_dtypes.bfloat16)
    low = (table - high.astype(np.float32)).astype(ml_dtypes.bfloat16)
    return np.block([[high, low], [high, np.zeros_like(low)]])


def azimuth_table():
    rows = np.arange(8)
    shifts = np.stack([DERIV[rows, (rows + d) % 8] for d in range(8)])
    return np.broadcast_to(shifts[:, :, None], (8, 8, 128)).astype(np.float32)


SIGNS = [
    (sx, sy, sz)
    for sx in (-1, 0, 1)
    for sy in (-1, 0, 1)
    for sz in (-1, 0, 1)
    if (sx, sy, sz) != (0, 0, 0)
]


def kernel(
    sizes,
    scalar_h,
    vel_h,
    mass_h,
    wts_h,
    cut_h,
    blk_h,
    tab_h,
    azi_h,
    adv_h,
    img_h,
    fld,
    vel,
    mass,
    wts,
    cut,
    blk,
    tab,
    azi,
    g_ref,
    first,
    winv,
    radial,
    adv,
    plane,
    rows,
    cols,
    lines,
    r_plane,
    r_rows,
    r_cols,
    r_xy,
    r_xz,
    r_yz,
    r_xyz,
    xcol,
    wide,
    wts_p,
    cut_hot,
    img_hot,
    elems,
    v_send,
    v_recv,
    blk_recv,
    img,
    in_sem,
    vel_sem,
    out_sem,
    send_sem,
    recv_sem,
    v_send_sem,
    v_recv_sem,
    b_send_sem,
    b_recv_sem,
):
    n_cam, n_ex, n_ey = sizes
    cam, ex, ey = lax.axis_index("cam"), lax.axis_index("ex"), lax.axis_index("ey")

    def peer(sx, sy, sz):
        return {
            "cam": lax.rem(cam + (sz + n_cam), n_cam),
            "ex": lax.rem(ex + (sx + n_ex), n_ex),
            "ey": lax.rem(ey + (sy + n_ey), n_ey),
        }

    def load(src, dst, sem):
        copy = pltpu.make_async_copy(src, dst, sem)
        copy.start()
        return copy

    load_mass = load(mass_h, mass, in_sem.at[0])
    load_fld = load(scalar_h, fld, in_sem.at[1])
    load_tab = load(tab_h, tab, in_sem.at[2])
    load_azi = load(azi_h, azi, in_sem.at[3])
    for a in range(4):
        load(vel_h.at[:, pl.ds(8 * a, 8)], vel.at[:, pl.ds(8 * a, 8)], vel_sem.at[a])
    load_blk = load(blk_h, blk, in_sem.at[4])
    load_cut = load(cut_h, cut, in_sem.at[5])
    load_wts = load(wts_h, wts, in_sem.at[6])

    barrier = pltpu.get_barrier_semaphore()
    for s in SIGNS:
        pl.semaphore_signal(barrier, inc=1, device_id=peer(*s), device_id_type=pl.DeviceIdType.MESH)
    for d in range(2, n_cam - 1):
        pl.semaphore_signal(
            barrier, inc=1, device_id=peer(0, 0, d), device_id_type=pl.DeviceIdType.MESH
        )

    lane = lax.broadcasted_iota(jnp.int32, (8, 128), 1)
    sub = lax.broadcasted_iota(jnp.int32, (8, 128), 0)
    even = lane % 2 == 0
    take_next = (lane % 8 == 7) & (lane != 127)
    take_prev = (lane % 8 == 0) & (lane != 0)
    edge = (lane == 0) | (lane == 127)
    zero = jnp.zeros((8, 128), F32)

    def lane_pairs(g):
        return (
            g
            + jnp.where(take_next, pltpu.roll(g, 127, 1), zero)
            + jnp.where(take_prev, pltpu.roll(g, 1, 1), zero)
        )

    copies = []

    def send(src, dst, e, s):
        which = e * 26 + SIGNS.index(s)
        copy = pltpu.make_async_remote_copy(
            src_ref=src,
            dst_ref=dst,
            send_sem=send_sem.at[which],
            recv_sem=recv_sem.at[which],
            device_id=peer(*s),
            device_id_type=pl.DeviceIdType.MESH,
        )
        copy.start()
        copies.append(copy)
        return copy

    def gather_faces(ref, e, wait_entry):
        @pl.loop(0, 4)
        def _(a):
            for i in range(8):
                n = 8 * a + i
                both = ref[n, pl.ds(7, 7, stride=8), :] + ref[n, pl.ds(8, 7, stride=8), :]
                ref[n, pl.ds(7, 7, stride=8), :] = both
                ref[n, pl.ds(8, 7, stride=8), :] = both

        for a in range(3):
            both = ref[8 * a + 7] + ref[8 * a + 8]
            ref[8 * a + 7] = both
            ref[8 * a + 8] = both
        plane[e, 0] = ref[0]
        plane[e, 1] = ref[31]
        wait_entry()
        started = []
        for px in (0, 1):
            started.append(send(plane.at[e, px], r_plane.at[e, px], e, (2 * px - 1, 0, 0)))
            for py in (0, 1):
                started.append(
                    send(
                        plane.at[e, px, pl.ds(56 * py, 8)],
                        r_xy.at[e, px, py],
                        e,
                        (2 * px - 1, 2 * py - 1, 0),
                    )
                )
        for n in range(32):
            rows[e, 0, n : n + 1, :] = ref[n, 0:1, :]
            rows[e, 1, n : n + 1, :] = ref[n, 63:64, :]
        for py in (0, 1):
            started.append(send(rows.at[e, py], r_rows.at[e, py], e, (0, 2 * py - 1, 0)))

        @pl.loop(0, 4)
        def _(a):
            acc = zero
            for i in range(8):
                for b in range(8):
                    spot = 8 * i + b
                    moved = pltpu.roll(ref[8 * a + i, 8 * b : 8 * b + 8, :], 2 * spot + 1, 1)
                    acc = jnp.where((lane == 2 * spot) | (lane == 2 * spot + 1), moved, acc)
            cols[e, a] = acc

        low, high = zero, zero
        for a in range(4):
            low = jnp.where(sub == a, jnp.broadcast_to(cols[e, a, 0:1, :], (8, 128)), low)
            high = jnp.where(sub == a, jnp.broadcast_to(cols[e, a, 7:8, :], (8, 128)), high)
        lines[e, 0] = low
        lines[e, 1] = high
        for pz in (0, 1):
            sz = 2 * pz - 1
            started.append(send(cols.at[e], r_cols.at[e, pz], e, (0, 0, sz)))
            for px in (0, 1):
                started.append(
                    send(cols.at[e, 3 * px], r_xz.at[e, px, pz], e, (2 * px - 1, 0, sz))
                )
                for py in (0, 1):
                    started.append(
                        send(
                            lines.at[e, py],
                            r_xyz.at[e, px, py, pz],
                            e,
                            (2 * px - 1, 2 * py - 1, sz),
                        )
                    )
            for py in (0, 1):
                started.append(send(lines.at[e, py], r_yz.at[e, py, pz], e, (0, 2 * py - 1, sz)))
        return started

    def add_faces(ref, e, started):
        for copy in started:
            copy.wait_recv()
        ref[0] = ref[0] + r_plane[e, 1]
        ref[31] = ref[31] + r_plane[e, 0]
        for n in range(32):
            ref[n, 0:1, :] = ref[n, 0:1, :] + r_rows[e, 1, n : n + 1, :]
            ref[n, 63:64, :] = ref[n, 63:64, :] + r_rows[e, 0, n : n + 1, :]
        for px in (0, 1):
            for py in (0, 1):
                n, row, got = (0 if px else 31), (0 if py else 63), (7 if py else 0)
                ref[n, row : row + 1, :] = (
                    ref[n, row : row + 1, :] + r_xy[e, px, py, got : got + 1, :]
                )
        across = []
        for py in (0, 1):
            t = jnp.where(even, r_yz[e, py, 1], r_yz[e, py, 0])
            for px in (0, 1):
                c = jnp.where(even, r_xyz[e, px, py, 1], r_xyz[e, px, py, 0])
                if px:
                    c = pltpu.roll(pltpu.roll(c, 16, 1), 5, 0)
                    t = t + jnp.where((lane < 16) & (sub == 0), c, zero)
                else:
                    c = pltpu.roll(pltpu.roll(c, 112, 1), 3, 0)
                    t = t + jnp.where((lane >= 112) & (sub == 3), c, zero)
            t = pltpu.roll(t, 114 if py else 14, 1)
            t = jnp.where((lane % 16 < 2) if py else (lane % 16 >= 14), t, zero)
            across.append(t)
        from_upper = jnp.where(cam < n_cam - 1, 1.0, 0.0).astype(F32)
        from_lower = jnp.where(cam > 0, 1.0, 0.0).astype(F32)
        keep = jnp.where(even, jnp.full((8, 128), from_upper), jnp.full((8, 128), from_lower))
        for a in range(4):
            q = jnp.where(even, r_cols[e, 1, a], r_cols[e, 0, a])
            q = q + jnp.where(sub == 0, jnp.broadcast_to(across[1][a : a + 1, :], (8, 128)), zero)
            q = q + jnp.where(sub == 7, jnp.broadcast_to(across[0][a : a + 1, :], (8, 128)), zero)
            if a == 0:
                c = jnp.where(even, r_xz[e, 1, 1], r_xz[e, 1, 0])
                q = q + jnp.where(lane < 16, pltpu.roll(c, 16, 1), zero)
            if a == 3:
                c = jnp.where(even, r_xz[e, 0, 1], r_xz[e, 0, 0])
                q = q + jnp.where(lane >= 112, pltpu.roll(c, 112, 1), zero)
            x = jnp.where(even, pltpu.roll(q, 127, 1), pltpu.roll(q, 1, 1))
            xcol[a] = x * keep

    def total(ref, x, n, i, b):
        spot = 8 * i + b
        return ref[n, 8 * b : 8 * b + 8, :] + jnp.where(
            edge, pltpu.roll(x, 127 - 2 * spot, 1), zero
        )

    def convect(src, a):
        block = src[pl.ds(8 * a, 8)].reshape(512, 128)
        high = block.astype(BF16)
        low = (block - high.astype(F32)).astype(BF16)
        both = jnp.dot(
            jnp.concatenate([high, low], axis=1), tab[...], preferred_element_type=F32
        )
        radial[...] = (both[:, :128] + both[:, 128:]).reshape(8, 64, 128)
        for b in range(8):
            part = slice(8 * b, 8 * b + 8)
            f = [src[8 * a + i, part, :] for i in range(8)]
            plus = [f[p] + f[7 - p] for p in range(4)]
            minus = [f[p] - f[7 - p] for p in range(4)]
            axial = [None] * 8
            for i in range(4):
                x = y = None
                for p in range(4):
                    alpha = float((DERIV[i, p] + DERIV[i, 7 - p]) / 2)
                    beta = float((DERIV[i, p] - DERIV[i, 7 - p]) / 2)
                    x = alpha * plus[p] if x is None else x + alpha * plus[p]
                    y = beta * minus[p] if y is None else y + beta * minus[p]
                axial[i] = x + y
                axial[7 - i] = y - x
            for i in range(8):
                n = 8 * a + i
                turned = azi[0] * f[i]
                for d in range(1, 8):
                    turned = turned + azi[d] * pltpu.roll(f[i], 8 - d, 0)
                c = (
                    vel[0, n, part, :] * axial[i]
                    + vel[1, n, part, :] * turned
                    + vel[2, n, part, :] * radial[i, part, :]
                )
                g_ref[n, part, :] = lane_pairs(mass[n, part, :] * c)

    load_mass.wait()

    @pl.loop(0, 4)
    def _(a):
        for i in range(8):
            for b in range(8):
                n, part = 8 * a + i, slice(8 * b, 8 * b + 8)
                winv[n, part, :] = lane_pairs(mass[n, part, :])

    sent_mass = gather_faces(winv, 0, lambda: pl.semaphore_wait(barrier, 26 + n_cam - 3))

    load_blk.wait()
    blk_copies = []
    for d in range(1, n_cam):
        copy = pltpu.make_async_remote_copy(
            src_ref=blk,
            dst_ref=blk_recv.at[d],
            send_sem=b_send_sem.at[d],
            recv_sem=b_recv_sem.at[d],
            device_id=peer(0, 0, d),
            device_id_type=pl.DeviceIdType.MESH,
        )
        copy.start()
        blk_copies.append(copy)

    load_fld.wait()
    load_tab.wait()
    load_azi.wait()

    @pl.loop(0, 4)
    def _(a):
        part = pl.ds(pl.multiple_of(8 * a, 8), 8)
        pltpu.make_async_copy(vel_h.at[:, part], vel.at[:, part], vel_sem.at[a]).wait()
        convect(fld, a)

    sent_one = gather_faces(g_ref, 1, lambda: None)

    add_faces(winv, 0, sent_mass)

    @pl.loop(0, 4)
    def _(a):
        x = xcol[a]
        for i in range(8):
            for b in range(8):
                n = 8 * a + i
                winv[n, 8 * b : 8 * b + 8, :] = -STEP / total(winv, x, n, i, b)

    add_faces(g_ref, 1, sent_one)

    @pl.loop(0, 4)
    def _(a):
        x = xcol[a]
        for i in range(8):
            for b in range(8):
                n, part = 8 * a + i, slice(8 * b, 8 * b + 8)
                first[n, part, :] = fld[n, part, :] + winv[n, part, :] * total(g_ref, x, n, i, b)
        convect(first, a)

    sent_two = gather_faces(g_ref, 2, lambda: None)

    load_cut.wait()
    load_wts.wait()

    @pl.loop(0, 8)
    def _(m):
        wide[...] = wts[m].astype(F32)
        for k in range(8):
            wts_p[m, 64 * k : 64 * k + 64, :] = wide[pl.ds(k, 64, stride=8), :].astype(BF16)
        chosen = jnp.broadcast_to(cut[pl.ds(m, 1), :].astype(F32), (128, 128)).T
        place = lax.broadcasted_iota(jnp.int32, (128, 128), 1).astype(F32)
        for q in range(4):
            cut_hot[m, :, 128 * q : 128 * q + 128] = jnp.where(
                chosen == place + 128.0 * q, 1.0, 0.0
            ).astype(BF16)

    for copy in blk_copies:
        copy.wait_recv()
    for d in range(n_cam):
        for t in range(2):
            if d == 0:
                ids = blk[pl.ds(2 * cam + t, 1), :]
            else:
                ids = blk_recv[d, pl.ds(2 * cam + t, 1), :]
            ids = jnp.broadcast_to(ids, (128, 128))
            for h in range(8):
                block_id = lax.broadcasted_iota(jnp.int32, (128, 128), 0) + 128 * h
                img_hot[t, 128 * h : 128 * h + 128, 128 * d : 128 * d + 128] = jnp.where(
                    ids == block_id, 1.0, 0.0
                ).astype(BF16)

    add_faces(g_ref, 2, sent_two)

    wide_lane = lax.broadcasted_iota(jnp.int32, (64, 128), 1)
    row64 = lax.broadcasted_iota(jnp.int32, (64, 128), 0)
    select = jnp.where(
        (wide_lane // 8 == row64 % 16) & ((wide_lane % 8) // 2 == row64 // 16), 1.0, 0.0
    ).astype(BF16)

    @pl.loop(0, 4)
    def _(a):
        x = xcol[a]
        for i in range(8):
            for b in range(8):
                n, part = 8 * a + i, slice(8 * b, 8 * b + 8)
                second = first[n, part, :] + winv[n, part, :] * total(g_ref, x, n, i, b)
                adv[n, part, :] = 0.5 * (fld[n, part, :] + second)
        part = pl.ds(pl.multiple_of(8 * a, 8), 8)
        pltpu.make_async_copy(adv.at[part], adv_h.at[part], out_sem.at[a]).start()
        for b in range(0, 8, 2):
            pieces = []
            for c in (b, b + 1):
                block = adv[pl.ds(8 * a, 8), 8 * c : 8 * c + 8, :].reshape(64, 128)
                pieces.append(jnp.where(wide_lane % 2 == 0, block, 0.0).astype(BF16))
                pieces.append(jnp.where(wide_lane % 2 == 1, block, 0.0).astype(BF16))
            out = lax.dot_general(
                select,
                jnp.concatenate(pieces, axis=0),
                (((1,), (1,)), ((), ())),
                preferred_element_type=F32,
            ).astype(BF16)
            for c in (0, 1):
                at = pl.multiple_of(128 * a + 16 * (b + c), 16)
                for h in range(4):
                    elems[pl.ds(at, 16), 128 * h : 128 * h + 128] = out[
                        16 * h : 16 * h + 16, 128 * c : 128 * c + 128
                    ]

    v_copies = []
    for d in list(range(1, n_cam)) + [0]:
        q = lax.rem(cam + d, n_cam)
        for t in range(2):
            m = 2 * q + t
            picked = jnp.dot(cut_hot[m], elems[...], preferred_element_type=F32).astype(BF16)
            value = jnp.dot(picked, wts_p[m], preferred_element_type=F32).astype(BF16)
            if d:
                v_send[d, t] = value
            else:
                v_recv[0, t] = value
        if d:
            copy = pltpu.make_async_remote_copy(
                src_ref=v_send.at[d],
                dst_ref=v_recv.at[d],
                send_sem=v_send_sem.at[d],
                recv_sem=v_recv_sem.at[d],
                device_id=peer(0, 0, d),
                device_id_type=pl.DeviceIdType.MESH,
            )
            copy.start()
            v_copies.append(copy)

    for copy in v_copies:
        copy.wait_recv()
    for t in range(2):
        values = jnp.concatenate([v_recv[d, t] for d in range(n_cam)], axis=0)
        img[t] = jnp.dot(img_hot[t], values, preferred_element_type=F32)
        pltpu.make_async_copy(img.at[t], img_h.at[t], out_sem.at[4 + t]).start()

    for copy in copies + blk_copies + v_copies:
        copy.wait_send()
    for a in range(4):
        part = pl.ds(8 * a, 8)
        pltpu.make_async_copy(adv.at[part], adv_h.at[part], out_sem.at[a]).wait()
    for t in range(2):
        pltpu.make_async_copy(img.at[t], img_h.at[t], out_sem.at[4 + t]).wait()


def per_device(sizes, scalar, velocity, lumped_mass, pixel_weights, cut_element, pixel_block):
    n_cam = sizes[0]
    flat = (32, 64, 128)
    hbm = pl.BlockSpec(memory_space=pl.ANY)
    big = pltpu.VMEM(flat, F32)
    dma = pltpu.SemaphoreType.DMA
    advected, images = pl.pallas_call(
        functools.partial(kernel, sizes),
        out_shape=(
            jax.ShapeDtypeStruct(flat, F32),
            jax.ShapeDtypeStruct((2, NBLK, 128), F32),
        ),
        in_specs=[hbm] * 8,
        out_specs=(hbm, hbm),
        scratch_shapes=[
            big,
            pltpu.VMEM((3,) + flat, F32),
            big,
            pltpu.VMEM((8, 512, 128), BF16),
            pltpu.VMEM((8, 128), jnp.int32),
            pltpu.VMEM((8, 128), jnp.int32),
            pltpu.VMEM((256, 256), BF16),
            pltpu.VMEM((8, 8, 128), F32),
            big,
            big,
            big,
            pltpu.VMEM((8, 64, 128), F32),
            big,
            pltpu.VMEM((3, 2, 64, 128), F32),
            pltpu.VMEM((3, 2, 32, 128), F32),
            pltpu.VMEM((3, 4, 8, 128), F32),
            pltpu.VMEM((3, 2, 8, 128), F32),
            pltpu.VMEM((3, 2, 64, 128), F32),
            pltpu.VMEM((3, 2, 32, 128), F32),
            pltpu.VMEM((3, 2, 4, 8, 128), F32),
            pltpu.VMEM((3, 2, 2, 8, 128), F32),
            pltpu.VMEM((3, 2, 2, 8, 128), F32),
            pltpu.VMEM((3, 2, 2, 8, 128), F32),
            pltpu.VMEM((3, 2, 2, 2, 8, 128), F32),
            pltpu.VMEM((4, 8, 128), F32),
            pltpu.VMEM((512, 128), F32),
            pltpu.VMEM((8, 512, 128), BF16),
            pltpu.VMEM((8, 128, 512), BF16),
            pltpu.VMEM((2, NBLK, 128 * n_cam), BF16),
            pltpu.VMEM((512, 512), BF16),
            pltpu.VMEM((n_cam, 2, 128, 128), BF16),
            pltpu.VMEM((n_cam, 2, 128, 128), BF16),
            pltpu.VMEM((n_cam, 8, 128), jnp.int32),
            pltpu.VMEM((2, NBLK, 128), F32),
            dma((7,)),
            dma((4,)),
            dma((6,)),
            dma((78,)),
            dma((78,)),
            dma((n_cam,)),
            dma((n_cam,)),
            dma((n_cam,)),
            dma((n_cam,)),
        ],
        compiler_params=pltpu.CompilerParams(
            collective_id=0, has_side_effects=True, vmem_limit_bytes=48 * 1024 * 1024
        ),
    )(
        scalar.reshape(flat),
        velocity.reshape((3,) + flat),
        lumped_mass.reshape(flat),
        pixel_weights,
        cut_element,
        pixel_block,
        jnp.asarray(radial_matrix()),
        jnp.asarray(azimuth_table()),
    )
    return advected.reshape(scalar.shape), images


def solution(mesh):
    sizes = tuple(mesh.shape[name] for name in ("cam", "ex", "ey"))
    placed = (
        P("ex", None, "ey", None, "cam"),
        P(None, "ex", None, "ey", None, "cam"),
        P("ex", None, "ey", None, "cam"),
        P(),
        P(None, ("cam", "ex", "ey")),
        P(None, ("cam", "ex", "ey")),
    )
    return jax.shard_map(
        functools.partial(per_device, sizes),
        mesh=mesh,
        in_specs=placed,
        out_specs=(P("ex", None, "ey", None, "cam"), P("cam", ("ex", "ey"), None)),
        check_vma=False,
    )
```

time: 192 us -> 49.5 us (0.26)
  waiting for transfers between devices: 59.8 us -> 0 us
  local copies, waits for them, and re-layouts: 61.8 us -> 8.64 us
  Pallas kernels: 0 us -> 39.8 us
  starting transfers between devices: 26.6 us -> 0 us
  matrix products: 17.1 us -> 0 us
  between operations: 14.4 us -> 0.65 us
  other arithmetic: 11.5 us -> 0 us
    reduce_scatter x1 -> x0, waiting for transfers between devices: 47.8 us -> none  [per_device(): lax.psum_scatter(jnp.einsum('cbs,csx->cbx', onehot, values, precision=lax...]
    pallas_call x0 -> x1, Pallas kernels: none -> 39.8 us  [per_device(): pl.pallas_call(functools.partial(kernel, sizes), out_shape=(jax.ShapeDtyp...]
    ppermute x12 -> x0, starting transfers between devices: 26.5 us -> none  [the longest x6 14.2 us: padded(): after = lax.ppermute(initial, axis, down)]
    reshape x3 -> x0, local copies, waits for them, and re-layouts: 19.9 us -> none  [per_device(): elements = advected.astype(jnp.bfloat16).reshape(shape[0], 8, shape[2], 8...]
    dot_general x8 -> x0, matrix products: 17.1 us -> none  [the longest x2 6.33 us: convect(): jnp.einsum('pi,aibjz->apbjz', derivative, field, precision=lax.Precision....]
    slice x10 -> x0, local copies, waits for them, and re-layouts: 16.1 us -> none  [the longest x7 8.53 us: padded(): initial = lax.slice_in_dim(shard, 0, width, axis=dim)]
    ppermute x12 -> x0, waiting for transfers between devices: 12 us -> none  [the longest x6 7.68 us: padded(): after = lax.ppermute(initial, axis, down)]
    transpose x1 -> x0, local copies, waits for them, and re-layouts: 10.5 us -> none  [per_device(): elements = advected.astype(jnp.bfloat16).reshape(shape[0], 8, shape[2], 8...]
  transfers between devices with their start and end apart: 13 -> 0, of which waited for: 9 -> 0; matrix products, arithmetic and copies ran while one was open for 4% -> 0% of each run, Pallas kernels for 0% -> 0%
where the time goes in v1:
time: 49.5 us; the launch traced here: 49.1 us
  Pallas kernels  39.8 us (80%)
  local copies, waits for them, and re-layouts  8.64 us (17%)
  between operations  0.65 us (1%)
    pallas_call x1, Pallas kernels, per_device(): pl.pallas_call(functools.partial(kernel, sizes), out_shape=(jax.ShapeDtyp...  39.8 us
    unnamed x16, local copies, waits for them, and re-layouts  8.64 us

profile of v1, /device:TPU:1, one launch (start us, length us, event | category | flops | bytes accessed | tf_op | source)
XLA Modules:
  0.0 49.1 jit_solution(3666326376421461054)
XLA Ops:
  0.6 0.0 copy-start
  0.6 1.2 %copy-done = f32[4,8,8,8,128]{4,3,2,1,0:T(8,128)S(1)} copy-done((f32[4,8,8,8,128]{4,3,2,1,0:T(8,128)S(1)}, f32[4,8,8,8,128]{4,3,2,1,0:T(8,128)}, u32[]{:S(2)}) %copy-start) | copy-done | bytes 1048600
  1.9 0.0 copy-start.1
  1.9 1.2 %copy-done.1 = f32[4,8,8,8,128]{4,3,2,1,0:T(8,128)S(1)} copy-done((f32[4,8,8,8,128]{4,3,2,1,0:T(8,128)S(1)}, f32[4,8,8,8,128]{4,3,2,1,0:T(8,128)}, u32[]{:S(2)}) %copy-start.1) | copy-done | bytes 1048600
  3.1 0.0 copy-start.2
  3.1 1.2 %copy-done.2 = bf16[8,512,128]{2,1,0:T(8,128)(2,1)S(1)} copy-done((bf16[8,512,128]{2,1,0:T(8,128)(2,1)S(1)}, bf16[8,512,128]{2,1,0:T(8,128)(2,1)}, u32[]{:S(2)}) %copy-start.2) | copy-done | bytes 1048600
  4.3 0.0 copy-start.3
  4.3 0.9 %copy-done.3 = bf16[256,256]{1,0:T(8,128)(2,1)S(1)} copy-done((bf16[256,256]{1,0:T(8,128)(2,1)S(1)}, bf16[256,256]{1,0:T(8,128)(2,1)}, u32[]{:S(2)}) %copy-start.3) | copy-done | bytes 131096
  5.2 0.0 copy-start.4
  5.2 0.8 %copy-done.4 = f32[8,8,128]{2,1,0:T(8,128)S(1)} copy-done((f32[8,8,128]{2,1,0:T(8,128)S(1)}, f32[8,8,128]{2,1,0:T(8,128)}, u32[]{:S(2)}) %copy-start.4) | copy-done | bytes 32792
  6.0 0.0 copy-start.5
  6.0 0.7 %copy-done.5 = s32[8,128]{1,0:T(8,128)S(1)} copy-done((s32[8,128]{1,0:T(8,128)S(1)}, s32[8,128]{1,0:T(8,128)}, u32[]{:S(2)}) %copy-start.5) | copy-done | bytes 4120
  6.7 0.0 copy-start.6
  6.7 0.7 %copy-done.6 = s32[8,128]{1,0:T(8,128)S(1)} copy-done((s32[8,128]{1,0:T(8,128)S(1)}, s32[8,128]{1,0:T(8,128)}, u32[]{:S(2)}) %copy-start.6) | copy-done | bytes 4120
  7.3 39.8 %shard_map.95 = (f32[32,64,128]{2,1,0:T(8,128)S(1)}, f32[2,1024,128]{2,1,0:T(8,128)S(1)}) custom-call(f32[32,64,128]{2,1,0:T(8,128)S(1)} %bitcast.4, f32[3,32,64,128]{3,2,1,0:T(8,128)} %bitcast.7, f32[32,64,128]{2,1,0:T(8,128)S(1)} %bitcast.5, bf16[8,512,128]{2,1,0:T(8,128)(2,1)S(1)} %copy-done.2, s32[8,128]{1,0:T(8,128)S(1)} %copy-done.5, ...), custom_call_target="tpu_custom_call" | custom-call | tf_op jit(solution)/shard_map/pallas_call | solution.py:527
  47.2 1.0 %copy.12 = f32[4,8,8,8,128]{4,3,2,1,0:T(8,128)} copy(f32[4,8,8,8,128]{4,3,2,1,0:T(8,128)S(1)} %bitcast.6) | data formatting | bytes 2097152
  48.2 1.0 %copy.13 = f32[2,1024,128]{2,1,0:T(8,128)} copy(f32[2,1024,128]{2,1,0:T(8,128)S(1)} %get-tuple-element.9) | data formatting | bytes 2097152
Async XLA Ops:
  0.6 1.2 %copy-start = (f32[4,8,8,8,128]{4,3,2,1,0:T(8,128)S(1)}, f32[4,8,8,8,128]{4,3,2,1,0:T(8,128)}, u32[]{:S(2)}) copy-start(f32[4,8,8,8,128]{4,3,2,1,0:T(8,128)} %param.8) | copy-start | bytes 3145732
  1.9 1.2 %copy-start.1 = (f32[4,8,8,8,128]{4,3,2,1,0:T(8,128)S(1)}, f32[4,8,8,8,128]{4,3,2,1,0:T(8,128)}, u32[]{:S(2)}) copy-start(f32[4,8,8,8,128]{4,3,2,1,0:T(8,128)} %param.10) | copy-start | bytes 3145732
  3.1 1.2 %copy-start.2 = (bf16[8,512,128]{2,1,0:T(8,128)(2,1)S(1)}, bf16[8,512,128]{2,1,0:T(8,128)(2,1)}, u32[]{:S(2)}) copy-start(bf16[8,512,128]{2,1,0:T(8,128)(2,1)} %wts_h.1) | copy-start | bytes 3145732
  4.3 0.9 %copy-start.3 = (bf16[256,256]{1,0:T(8,128)(2,1)S(1)}, bf16[256,256]{1,0:T(8,128)(2,1)}, u32[]{:S(2)}) copy-start(bf16[256,256]{1,0:T(8,128)(2,1)} %constant.4.clone.tab_h) | copy-start | bytes 393220
  5.2 0.8 %copy-start.4 = (f32[8,8,128]{2,1,0:T(8,128)S(1)}, f32[8,8,128]{2,1,0:T(8,128)}, u32[]{:S(2)}) copy-start(f32[8,8,128]{2,1,0:T(8,128)} %constant.5.clone.azi_h) | copy-start | bytes 98308
  6.0 0.7 %copy-start.5 = (s32[8,128]{1,0:T(8,128)S(1)}, s32[8,128]{1,0:T(8,128)}, u32[]{:S(2)}) copy-start(s32[8,128]{1,0:T(8,128)} %cut_h.1) | copy-start | bytes 12292
  6.7 0.7 %copy-start.6 = (s32[8,128]{1,0:T(8,128)S(1)}, s32[8,128]{1,0:T(8,128)}, u32[]{:S(2)}) copy-start(s32[8,128]{1,0:T(8,128)} %blk_h.1) | copy-start | bytes 12292

commit v2 on v1

--- a/solution.py
+++ b/solution.py
@@ -102,17 +102,8 @@
     winv,
     radial,
     adv,
-    plane,
-    rows,
-    cols,
-    lines,
-    r_plane,
-    r_rows,
-    r_cols,
-    r_xy,
-    r_xz,
-    r_yz,
-    r_xyz,
+    faces_one,
+    faces_two,
     xcol,
     wide,
     wts_p,
@@ -135,6 +126,7 @@
 ):
     n_cam, n_ex, n_ey = sizes
     cam, ex, ey = lax.axis_index("cam"), lax.axis_index("ex"), lax.axis_index("ey")
+    faces = (faces_one, faces_two)
 
     def peer(sx, sy, sz):
         return {
@@ -152,7 +144,7 @@
     load_fld = load(scalar_h, fld, in_sem.at[1])
     load_tab = load(tab_h, tab, in_sem.at[2])
     load_azi = load(azi_h, azi, in_sem.at[3])
-    for a in range(4):
+    for a in (0, 3, 1, 2):
         load(vel_h.at[:, pl.ds(8 * a, 8)], vel.at[:, pl.ds(8 * a, 8)], vel_sem.at[a])
     load_blk = load(blk_h, blk, in_sem.at[4])
     load_cut = load(cut_h, cut, in_sem.at[5])
@@ -173,6 +165,9 @@
     take_prev = (lane % 8 == 0) & (lane != 0)
     edge = (lane == 0) | (lane == 127)
     zero = jnp.zeros((8, 128), F32)
+    from_upper = jnp.where(cam < n_cam - 1, 1.0, 0.0).astype(F32)
+    from_lower = jnp.where(cam > 0, 1.0, 0.0).astype(F32)
+    keep = jnp.where(even, jnp.full((8, 128), from_upper), jnp.full((8, 128), from_lower))
 
     def lane_pairs(g):
         return (
@@ -181,9 +176,18 @@
             + jnp.where(take_prev, pltpu.roll(g, 1, 1), zero)
         )
 
+    def twice(body):
+        def outer(which):
+            @pl.loop(0, 2)
+            def _(t):
+                body(3 * t if which == "ends" else 1 + t)
+
+        return outer
+
     copies = []
-
-    def send(src, dst, e, s):
+    waits = {}
+
+    def send(src, dst, e, group, s):
         which = e * 26 + SIGNS.index(s)
         copy = pltpu.make_async_remote_copy(
             src_ref=src,
@@ -195,121 +199,135 @@
         )
         copy.start()
         copies.append(copy)
-        return copy
-
-    def gather_faces(ref, e, wait_entry):
-        @pl.loop(0, 4)
-        def _(a):
-            for i in range(8):
-                n = 8 * a + i
-                both = ref[n, pl.ds(7, 7, stride=8), :] + ref[n, pl.ds(8, 7, stride=8), :]
-                ref[n, pl.ds(7, 7, stride=8), :] = both
-                ref[n, pl.ds(8, 7, stride=8), :] = both
-
+        waits.setdefault((e, group), []).append(copy)
+
+    def wait_for(e, group):
+        for copy in waits[e, group]:
+            copy.wait_recv()
+
+    def pair_azimuth(ref, a):
+        for i in range(8):
+            n = 8 * a + i
+            both = ref[n, pl.ds(7, 7, stride=8), :] + ref[n, pl.ds(8, 7, stride=8), :]
+            ref[n, pl.ds(7, 7, stride=8), :] = both
+            ref[n, pl.ds(8, 7, stride=8), :] = both
+
+    def pair_axial(ref):
         for a in range(3):
             both = ref[8 * a + 7] + ref[8 * a + 8]
             ref[8 * a + 7] = both
             ref[8 * a + 8] = both
-        plane[e, 0] = ref[0]
-        plane[e, 1] = ref[31]
-        wait_entry()
-        started = []
+
+    def gather_columns(pieces):
+        parts = [zero] * 4
+        for at, (spot, piece) in enumerate(pieces):
+            here = (lane == 2 * spot) | (lane == 2 * spot + 1)
+            parts[at % 4] = jnp.where(here, pltpu.roll(piece, 2 * spot + 1, 1), parts[at % 4])
+        return (parts[0] + parts[1]) + (parts[2] + parts[3])
+
+    def pack_ends(ref, e, kind):
+        plane, tile = faces[e][0], faces[e][1]
         for px in (0, 1):
-            started.append(send(plane.at[e, px], r_plane.at[e, px], e, (2 * px - 1, 0, 0)))
+            plane[px, kind] = ref[31 * px]
+            tile[px, kind] = gather_columns(
+                [(56 * px + b, ref[31 * px, 8 * b : 8 * b + 8, :]) for b in range(8)]
+            )
+
+    def send_ends(e):
+        plane, tile, _, _, _, r_plane, r_xy, r_xz, r_xyz, _, _, _ = faces[e]
+        for px in (0, 1):
+            sx = 2 * px - 1
+            send(plane.at[px], r_plane.at[px], e, "ends", (sx, 0, 0))
             for py in (0, 1):
-                started.append(
-                    send(
-                        plane.at[e, px, pl.ds(56 * py, 8)],
-                        r_xy.at[e, px, py],
-                        e,
-                        (2 * px - 1, 2 * py - 1, 0),
-                    )
+                send(
+                    plane.at[px, :, pl.ds(56 * py, 8)],
+                    r_xy.at[px, py],
+                    e,
+                    "ends",
+                    (sx, 2 * py - 1, 0),
                 )
+            for pz in (0, 1):
+                sz = 2 * pz - 1
+                send(tile.at[px], r_xz.at[px, pz], e, "ends", (sx, 0, sz))
+                for py in (0, 1):
+                    send(tile.at[px], r_xyz.at[px, py, pz], e, "ends", (sx, 2 * py - 1, sz))
+
+    def pack_rest(ref, e, kind):
+        rows, cols, lines = faces[e][2:5]
         for n in range(32):
-            rows[e, 0, n : n + 1, :] = ref[n, 0:1, :]
-            rows[e, 1, n : n + 1, :] = ref[n, 63:64, :]
-        for py in (0, 1):
-            started.append(send(rows.at[e, py], r_rows.at[e, py], e, (0, 2 * py - 1, 0)))
+            rows[0, kind, n : n + 1, :] = ref[n, 0:1, :]
+            rows[1, kind, n : n + 1, :] = ref[n, 63:64, :]
 
         @pl.loop(0, 4)
         def _(a):
-            acc = zero
-            for i in range(8):
-                for b in range(8):
-                    spot = 8 * i + b
-                    moved = pltpu.roll(ref[8 * a + i, 8 * b : 8 * b + 8, :], 2 * spot + 1, 1)
-                    acc = jnp.where((lane == 2 * spot) | (lane == 2 * spot + 1), moved, acc)
-            cols[e, a] = acc
+            cols[a, kind] = gather_columns(
+                [
+                    (8 * i + b, ref[8 * a + i, 8 * b : 8 * b + 8, :])
+                    for i in range(8)
+                    for b in range(8)
+                ]
+            )
 
         low, high = zero, zero
         for a in range(4):
-            low = jnp.where(sub == a, jnp.broadcast_to(cols[e, a, 0:1, :], (8, 128)), low)
-            high = jnp.where(sub == a, jnp.broadcast_to(cols[e, a, 7:8, :], (8, 128)), high)
-        lines[e, 0] = low
-        lines[e, 1] = high
+            low = jnp.where(sub == a, jnp.broadcast_to(cols[a, kind, 0:1, :], (8, 128)), low)
+            high = jnp.where(sub == a, jnp.broadcast_to(cols[a, kind, 7:8, :], (8, 128)), high)
+        lines[0, kind] = low
+        lines[1, kind] = high
+
+    def send_rest(e):
+        rows, cols, lines = faces[e][2:5]
+        r_rows, r_cols, r_yz = faces[e][9:12]
         for pz in (0, 1):
             sz = 2 * pz - 1
-            started.append(send(cols.at[e], r_cols.at[e, pz], e, (0, 0, sz)))
-            for px in (0, 1):
-                started.append(
-                    send(cols.at[e, 3 * px], r_xz.at[e, px, pz], e, (2 * px - 1, 0, sz))
-                )
-                for py in (0, 1):
-                    started.append(
-                        send(
-                            lines.at[e, py],
-                            r_xyz.at[e, px, py, pz],
-                            e,
-                            (2 * px - 1, 2 * py - 1, sz),
-                        )
-                    )
+            send(cols, r_cols.at[pz], e, "rest", (0, 0, sz))
             for py in (0, 1):
-                started.append(send(lines.at[e, py], r_yz.at[e, py, pz], e, (0, 2 * py - 1, sz)))
-        return started
-
-    def add_faces(ref, e, started):
-        for copy in started:
-            copy.wait_recv()
-        ref[0] = ref[0] + r_plane[e, 1]
-        ref[31] = ref[31] + r_plane[e, 0]
+                send(lines.at[py], r_yz.at[py, pz], e, "rest", (0, 2 * py - 1, sz))
+        for py in (0, 1):
+            send(rows.at[py], r_rows.at[py], e, "rest", (0, 2 * py - 1, 0))
+
+    def across_azimuth(t, py):
+        t = pltpu.roll(t, 114 if py else 14, 1)
+        return jnp.where((lane % 16 < 2) if py else (lane % 16 >= 14), t, zero)
+
+    def swap(q):
+        return jnp.where(even, pltpu.roll(q, 127, 1), pltpu.roll(q, 1, 1)) * keep
+
+    def add_rest(ref, e, kind):
+        r_rows, r_cols, r_yz = faces[e][9:12]
         for n in range(32):
-            ref[n, 0:1, :] = ref[n, 0:1, :] + r_rows[e, 1, n : n + 1, :]
-            ref[n, 63:64, :] = ref[n, 63:64, :] + r_rows[e, 0, n : n + 1, :]
-        for px in (0, 1):
-            for py in (0, 1):
-                n, row, got = (0 if px else 31), (0 if py else 63), (7 if py else 0)
-                ref[n, row : row + 1, :] = (
-                    ref[n, row : row + 1, :] + r_xy[e, px, py, got : got + 1, :]
-                )
-        across = []
-        for py in (0, 1):
-            t = jnp.where(even, r_yz[e, py, 1], r_yz[e, py, 0])
-            for px in (0, 1):
-                c = jnp.where(even, r_xyz[e, px, py, 1], r_xyz[e, px, py, 0])
-                if px:
-                    c = pltpu.roll(pltpu.roll(c, 16, 1), 5, 0)
-                    t = t + jnp.where((lane < 16) & (sub == 0), c, zero)
-                else:
-                    c = pltpu.roll(pltpu.roll(c, 112, 1), 3, 0)
-                    t = t + jnp.where((lane >= 112) & (sub == 3), c, zero)
-            t = pltpu.roll(t, 114 if py else 14, 1)
-            t = jnp.where((lane % 16 < 2) if py else (lane % 16 >= 14), t, zero)
-            across.append(t)
-        from_upper = jnp.where(cam < n_cam - 1, 1.0, 0.0).astype(F32)
-        from_lower = jnp.where(cam > 0, 1.0, 0.0).astype(F32)
-        keep = jnp.where(even, jnp.full((8, 128), from_upper), jnp.full((8, 128), from_lower))
+            ref[n, 0:1, :] = ref[n, 0:1, :] + r_rows[1, kind, n : n + 1, :]
+            ref[n, 63:64, :] = ref[n, 63:64, :] + r_rows[0, kind, n : n + 1, :]
+        across = [
+            across_azimuth(jnp.where(even, r_yz[py, 1, kind], r_yz[py, 0, kind]), py)
+            for py in (0, 1)
+        ]
         for a in range(4):
-            q = jnp.where(even, r_cols[e, 1, a], r_cols[e, 0, a])
+            q = jnp.where(even, r_cols[1, a, kind], r_cols[0, a, kind])
             q = q + jnp.where(sub == 0, jnp.broadcast_to(across[1][a : a + 1, :], (8, 128)), zero)
             q = q + jnp.where(sub == 7, jnp.broadcast_to(across[0][a : a + 1, :], (8, 128)), zero)
-            if a == 0:
-                c = jnp.where(even, r_xz[e, 1, 1], r_xz[e, 1, 0])
-                q = q + jnp.where(lane < 16, pltpu.roll(c, 16, 1), zero)
-            if a == 3:
-                c = jnp.where(even, r_xz[e, 0, 1], r_xz[e, 0, 0])
-                q = q + jnp.where(lane >= 112, pltpu.roll(c, 112, 1), zero)
-            x = jnp.where(even, pltpu.roll(q, 127, 1), pltpu.roll(q, 1, 1))
-            xcol[a] = x * keep
+            xcol[kind, a] = swap(q)
+
+    def add_ends(ref, e, kind):
+        r_plane, r_xy, r_xz, r_xyz = faces[e][5:9]
+        for px in (0, 1):
+            n, a = (0, 0) if px else (31, 3)
+            ref[n] = ref[n] + r_plane[px, kind]
+            for py in (0, 1):
+                row, got = (0, 7) if py else (63, 0)
+                ref[n, row : row + 1, :] = (
+                    ref[n, row : row + 1, :] + r_xy[px, py, kind, got : got + 1, :]
+                )
+            q = jnp.where(even, r_xz[px, 1, kind], r_xz[px, 0, kind])
+            for py in (0, 1):
+                c = jnp.where(even, r_xyz[px, py, 1, kind], r_xyz[px, py, 0, kind])
+                c = pltpu.roll(across_azimuth(c, py), 1 if py else 7, 0)
+                q = q + jnp.where(sub == (0 if py else 7), c, zero)
+            if px:
+                q = jnp.where(lane < 16, pltpu.roll(q, 16, 1), zero)
+            else:
+                q = jnp.where(lane >= 112, pltpu.roll(q, 112, 1), zero)
+            xcol[kind, a] = xcol[kind, a] + swap(q)
 
     def total(ref, x, n, i, b):
         spot = 8 * i + b
@@ -351,6 +369,7 @@
                     + vel[2, n, part, :] * radial[i, part, :]
                 )
                 g_ref[n, part, :] = lane_pairs(mass[n, part, :] * c)
+        pair_azimuth(g_ref, a)
 
     load_mass.wait()
 
@@ -360,8 +379,30 @@
             for b in range(8):
                 n, part = 8 * a + i, slice(8 * b, 8 * b + 8)
                 winv[n, part, :] = lane_pairs(mass[n, part, :])
-
-    sent_mass = gather_faces(winv, 0, lambda: pl.semaphore_wait(barrier, 26 + n_cam - 3))
+        pair_azimuth(winv, a)
+
+    pair_axial(winv)
+    pack_ends(winv, 0, 1)
+    pack_rest(winv, 0, 1)
+
+    load_fld.wait()
+    load_tab.wait()
+    load_azi.wait()
+
+    @twice
+    def stage_one(a):
+        part = pl.ds(pl.multiple_of(8 * a, 8), 8)
+        pltpu.make_async_copy(vel_h.at[:, part], vel.at[:, part], vel_sem.at[a]).wait()
+        convect(fld, a)
+
+    stage_one("ends")
+    pack_ends(g_ref, 0, 0)
+    pl.semaphore_wait(barrier, 26 + n_cam - 3)
+    send_ends(0)
+    stage_one("middle")
+    pair_axial(g_ref)
+    pack_rest(g_ref, 0, 0)
+    send_rest(0)
 
     load_blk.wait()
     blk_copies = []
@@ -377,41 +418,6 @@
         copy.start()
         blk_copies.append(copy)
 
-    load_fld.wait()
-    load_tab.wait()
-    load_azi.wait()
-
-    @pl.loop(0, 4)
-    def _(a):
-        part = pl.ds(pl.multiple_of(8 * a, 8), 8)
-        pltpu.make_async_copy(vel_h.at[:, part], vel.at[:, part], vel_sem.at[a]).wait()
-        convect(fld, a)
-
-    sent_one = gather_faces(g_ref, 1, lambda: None)
-
-    add_faces(winv, 0, sent_mass)
-
-    @pl.loop(0, 4)
-    def _(a):
-        x = xcol[a]
-        for i in range(8):
-            for b in range(8):
-                n = 8 * a + i
-                winv[n, 8 * b : 8 * b + 8, :] = -STEP / total(winv, x, n, i, b)
-
-    add_faces(g_ref, 1, sent_one)
-
-    @pl.loop(0, 4)
-    def _(a):
-        x = xcol[a]
-        for i in range(8):
-            for b in range(8):
-                n, part = 8 * a + i, slice(8 * b, 8 * b + 8)
-                first[n, part, :] = fld[n, part, :] + winv[n, part, :] * total(g_ref, x, n, i, b)
-        convect(first, a)
-
-    sent_two = gather_faces(g_ref, 2, lambda: None)
-
     load_cut.wait()
     load_wts.wait()
 
@@ -426,6 +432,31 @@
             cut_hot[m, :, 128 * q : 128 * q + 128] = jnp.where(
                 chosen == place + 128.0 * q, 1.0, 0.0
             ).astype(BF16)
+
+    @twice
+    def stage_two(a):
+        x, y = xcol[0, a], xcol[1, a]
+        for i in range(8):
+            for b in range(8):
+                n, part = 8 * a + i, slice(8 * b, 8 * b + 8)
+                factor = -STEP / total(winv, y, n, i, b)
+                winv[n, part, :] = factor
+                first[n, part, :] = fld[n, part, :] + factor * total(g_ref, x, n, i, b)
+        convect(first, a)
+
+    wait_for(0, "rest")
+    add_rest(winv, 0, 1)
+    add_rest(g_ref, 0, 0)
+    stage_two("middle")
+    wait_for(0, "ends")
+    add_ends(winv, 0, 1)
+    add_ends(g_ref, 0, 0)
+    stage_two("ends")
+    pack_ends(g_ref, 1, 0)
+    send_ends(1)
+    pair_axial(g_ref)
+    pack_rest(g_ref, 1, 0)
+    send_rest(1)
 
     for copy in blk_copies:
         copy.wait_recv()
@@ -442,17 +473,15 @@
                     ids == block_id, 1.0, 0.0
                 ).astype(BF16)
 
-    add_faces(g_ref, 2, sent_two)
-
     wide_lane = lax.broadcasted_iota(jnp.int32, (64, 128), 1)
     row64 = lax.broadcasted_iota(jnp.int32, (64, 128), 0)
     select = jnp.where(
         (wide_lane // 8 == row64 % 16) & ((wide_lane % 8) // 2 == row64 // 16), 1.0, 0.0
     ).astype(BF16)
 
-    @pl.loop(0, 4)
-    def _(a):
-        x = xcol[a]
+    @twice
+    def finish(a):
+        x = xcol[0, a]
         for i in range(8):
             for b in range(8):
                 n, part = 8 * a + i, slice(8 * b, 8 * b + 8)
@@ -479,8 +508,15 @@
                         16 * h : 16 * h + 16, 128 * c : 128 * c + 128
                     ]
 
+    wait_for(1, "rest")
+    add_rest(g_ref, 1, 0)
+    finish("middle")
+    wait_for(1, "ends")
+    add_ends(g_ref, 1, 0)
+    finish("ends")
+
     v_copies = []
-    for d in list(range(1, n_cam)) + [0]:
+    for d in sorted(range(1, n_cam), key=lambda d: -min(d, n_cam - d)) + [0]:
         q = lax.rem(cam + d, n_cam)
         for t in range(2):
             m = 2 * q + t
@@ -502,6 +538,8 @@
             copy.start()
             v_copies.append(copy)
 
+    for copy in copies + blk_copies:
+        copy.wait_send()
     for copy in v_copies:
         copy.wait_recv()
     for t in range(2):
@@ -509,7 +547,7 @@
         img[t] = jnp.dot(img_hot[t], values, preferred_element_type=F32)
         pltpu.make_async_copy(img.at[t], img_h.at[t], out_sem.at[4 + t]).start()
 
-    for copy in copies + blk_copies + v_copies:
+    for copy in v_copies:
         copy.wait_send()
     for a in range(4):
         part = pl.ds(8 * a, 8)
@@ -518,10 +556,28 @@
         pltpu.make_async_copy(img.at[t], img_h.at[t], out_sem.at[4 + t]).wait()
 
 
+def face_buffers(kinds):
+    shapes = [
+        (2, kinds, 64, 128),
+        (2, kinds, 8, 128),
+        (2, kinds, 32, 128),
+        (4, kinds, 8, 128),
+        (2, kinds, 8, 128),
+        (2, kinds, 64, 128),
+        (2, 2, kinds, 8, 128),
+        (2, 2, kinds, 8, 128),
+        (2, 2, 2, kinds, 8, 128),
+        (2, kinds, 32, 128),
+        (2, 4, kinds, 8, 128),
+        (2, 2, kinds, 8, 128),
+    ]
+    return tuple(pltpu.VMEM(shape, F32) for shape in shapes)
+
+
 def per_device(sizes, scalar, velocity, lumped_mass, pixel_weights, cut_element, pixel_block):
     n_cam = sizes[0]
     flat = (32, 64, 128)
-    hbm = pl.BlockSpec(memory_space=pl.ANY)
+    hbm = pl.BlockSpec(memory_space=pltpu.HBM)
     big = pltpu.VMEM(flat, F32)
     dma = pltpu.SemaphoreType.DMA
     advected, images = pl.pallas_call(
@@ -546,18 +602,9 @@
             big,
             pltpu.VMEM((8, 64, 128), F32),
             big,
-            pltpu.VMEM((3, 2, 64, 128), F32),
-            pltpu.VMEM((3, 2, 32, 128), F32),
-            pltpu.VMEM((3, 4, 8, 128), F32),
-            pltpu.VMEM((3, 2, 8, 128), F32),
-            pltpu.VMEM((3, 2, 64, 128), F32),
-            pltpu.VMEM((3, 2, 32, 128), F32),
-            pltpu.VMEM((3, 2, 4, 8, 128), F32),
-            pltpu.VMEM((3, 2, 2, 8, 128), F32),
-            pltpu.VMEM((3, 2, 2, 8, 128), F32),
-            pltpu.VMEM((3, 2, 2, 8, 128), F32),
-            pltpu.VMEM((3, 2, 2, 2, 8, 128), F32),
-            pltpu.VMEM((4, 8, 128), F32),
+            face_buffers(2),
+            face_buffers(1),
+            pltpu.VMEM((2, 4, 8, 128), F32),
             pltpu.VMEM((512, 128), F32),
             pltpu.VMEM((8, 512, 128), BF16),
             pltpu.VMEM((8, 128, 512), BF16),
@@ -570,15 +617,15 @@
             dma((7,)),
             dma((4,)),
             dma((6,)),
-            dma((78,)),
-            dma((78,)),
+            dma((52,)),
+            dma((52,)),
             dma((n_cam,)),
             dma((n_cam,)),
             dma((n_cam,)),
             dma((n_cam,)),
         ],
         compiler_params=pltpu.CompilerParams(
-            collective_id=0, has_side_effects=True, vmem_limit_bytes=48 * 1024 * 1024
+            collective_id=0, has_side_effects=True, vmem_limit_bytes=62 * 1024 * 1024
         ),
     )(
         scalar.reshape(flat),

time: 49.5 us -> 40.2 us (0.81)
  Pallas kernels: 39.8 us -> 34.8 us
  local copies, waits for them, and re-layouts: 8.64 us -> 4.57 us
    pallas_call x1, Pallas kernels: 39.8 us -> 34.8 us  [per_device(): pl.pallas_call(functools.partial(kernel, sizes), out_shape=(jax.ShapeDtyp...]
    unnamed x16 -> x2, local copies, waits for them, and re-layouts: 8.64 us -> 4.57 us
where the time goes in v2:
time: 40.2 us; the launch traced here: 40 us
  Pallas kernels  34.8 us (87%)
  local copies, waits for them, and re-layouts  4.57 us (11%)
  between operations  0.64 us (2%)
    pallas_call x1, Pallas kernels, per_device(): pl.pallas_call(functools.partial(kernel, sizes), out_shape=(jax.ShapeDtyp...  34.8 us
    unnamed x2, local copies, waits for them, and re-layouts  4.57 us

profile of v2, /device:TPU:1, one launch (start us, length us, event | category | flops | bytes accessed | tf_op | source)
XLA Modules:
  0.0 40.0 jit_solution(3268920451335294325)
XLA Ops:
  0.6 34.8 %shard_map.95 = (f32[32,64,128]{2,1,0:T(8,128)}, f32[2,1024,128]{2,1,0:T(8,128)}) custom-call(f32[32,64,128]{2,1,0:T(8,128)} %bitcast.5, f32[3,32,64,128]{3,2,1,0:T(8,128)} %bitcast.4, f32[32,64,128]{2,1,0:T(8,128)} %bitcast.6, bf16[8,512,128]{2,1,0:T(8,128)(2,1)} %wts_h.1, s32[8,128]{1,0:T(8,128)} %cut_h.1, s32[8,128]{1,0:T(8,128)} %blk_h.1, ...), custom_call_target="tpu_custom_call" | custom-call | tf_op jit(solution)/shard_map/pallas_call | solution.py:583
  35.4 2.3 %copy.12 = f32[4,8,8,8,128]{4,3,2,1,0:T(8,128)} copy(f32[4,8,8,8,128]{4,3,2,1,0:T(8,128)} %bitcast.7) | data formatting | bytes 2097152
  37.8 2.3 %copy.13 = f32[2,1024,128]{2,1,0:T(8,128)} copy(f32[2,1024,128]{2,1,0:T(8,128)} %get-tuple-element.9) | data formatting | bytes 2097152

commit v3 on v2

--- a/solution.py
+++ b/solution.py
@@ -87,8 +87,9 @@
     blk_h,
     tab_h,
     azi_h,
-    adv_h,
-    img_h,
+    adv,
+    v_recv,
+    img_hot,
     fld,
     vel,
     mass,
@@ -101,22 +102,17 @@
     first,
     winv,
     radial,
-    adv,
     faces_one,
     faces_two,
     xcol,
     wide,
     wts_p,
     cut_hot,
-    img_hot,
     elems,
     v_send,
-    v_recv,
     blk_recv,
-    img,
     in_sem,
     vel_sem,
-    out_sem,
     send_sem,
     recv_sem,
     v_send_sem,
@@ -487,8 +483,6 @@
                 n, part = 8 * a + i, slice(8 * b, 8 * b + 8)
                 second = first[n, part, :] + winv[n, part, :] * total(g_ref, x, n, i, b)
                 adv[n, part, :] = 0.5 * (fld[n, part, :] + second)
-        part = pl.ds(pl.multiple_of(8 * a, 8), 8)
-        pltpu.make_async_copy(adv.at[part], adv_h.at[part], out_sem.at[a]).start()
         for b in range(0, 8, 2):
             pieces = []
             for c in (b, b + 1):
@@ -542,18 +536,28 @@
         copy.wait_send()
     for copy in v_copies:
         copy.wait_recv()
-    for t in range(2):
-        values = jnp.concatenate([v_recv[d, t] for d in range(n_cam)], axis=0)
-        img[t] = jnp.dot(img_hot[t], values, preferred_element_type=F32)
-        pltpu.make_async_copy(img.at[t], img_h.at[t], out_sem.at[4 + t]).start()
-
     for copy in v_copies:
         copy.wait_send()
-    for a in range(4):
-        part = pl.ds(8 * a, 8)
-        pltpu.make_async_copy(adv.at[part], adv_h.at[part], out_sem.at[a]).wait()
+
+
+def write_kernel(adv, values, img_hot, adv_h, img_h, img, sem):
+    result = pltpu.make_async_copy(adv, adv_h, sem.at[0])
+    result.start()
+    n_cam = values.shape[0]
+    copies = []
     for t in range(2):
-        pltpu.make_async_copy(img.at[t], img_h.at[t], out_sem.at[4 + t]).wait()
+        slots = jnp.concatenate([values[d, t] for d in range(n_cam)], axis=0)
+        for h in range(2):
+            part = pl.ds(h * (NBLK // 2), NBLK // 2)
+            img[t, part] = jnp.dot(img_hot[t, part], slots, preferred_element_type=F32)
+            copy = pltpu.make_async_copy(
+                img.at[t, part], img_h.at[t, part], sem.at[1 + 2 * t + h]
+            )
+            copy.start()
+            copies.append(copy)
+    for copy in copies:
+        copy.wait()
+    result.wait()
 
 
 def face_buffers(kinds):
@@ -580,14 +584,27 @@
     hbm = pl.BlockSpec(memory_space=pltpu.HBM)
     big = pltpu.VMEM(flat, F32)
     dma = pltpu.SemaphoreType.DMA
-    advected, images = pl.pallas_call(
+    on_chip = pl.BlockSpec(memory_space=pltpu.VMEM)
+    outputs = (
+        pltpu.VMEM(flat, F32),
+        pltpu.VMEM((n_cam, 2, 128, 128), BF16),
+        pltpu.VMEM((2, NBLK, 128 * n_cam), BF16),
+    )
+    operands = (
+        scalar.reshape(flat),
+        velocity.reshape((3,) + flat),
+        lumped_mass.reshape(flat),
+        pixel_weights,
+        cut_element,
+        pixel_block,
+        jnp.asarray(radial_matrix()),
+        jnp.asarray(azimuth_table()),
+    )
+    results = pl.pallas_call(
         functools.partial(kernel, sizes),
-        out_shape=(
-            jax.ShapeDtypeStruct(flat, F32),
-            jax.ShapeDtypeStruct((2, NBLK, 128), F32),
-        ),
+        out_shape=outputs,
         in_specs=[hbm] * 8,
-        out_specs=(hbm, hbm),
+        out_specs=(on_chip,) * 3,
         scratch_shapes=[
             big,
             pltpu.VMEM((3,) + flat, F32),
@@ -601,22 +618,17 @@
             big,
             big,
             pltpu.VMEM((8, 64, 128), F32),
-            big,
             face_buffers(2),
             face_buffers(1),
             pltpu.VMEM((2, 4, 8, 128), F32),
             pltpu.VMEM((512, 128), F32),
             pltpu.VMEM((8, 512, 128), BF16),
             pltpu.VMEM((8, 128, 512), BF16),
-            pltpu.VMEM((2, NBLK, 128 * n_cam), BF16),
             pltpu.VMEM((512, 512), BF16),
             pltpu.VMEM((n_cam, 2, 128, 128), BF16),
-            pltpu.VMEM((n_cam, 2, 128, 128), BF16),
             pltpu.VMEM((n_cam, 8, 128), jnp.int32),
-            pltpu.VMEM((2, NBLK, 128), F32),
             dma((7,)),
             dma((4,)),
-            dma((6,)),
             dma((52,)),
             dma((52,)),
             dma((n_cam,)),
@@ -625,18 +637,20 @@
             dma((n_cam,)),
         ],
         compiler_params=pltpu.CompilerParams(
-            collective_id=0, has_side_effects=True, vmem_limit_bytes=62 * 1024 * 1024
+            collective_id=0, has_side_effects=True, vmem_limit_bytes=40 * 1024 * 1024
         ),
-    )(
-        scalar.reshape(flat),
-        velocity.reshape((3,) + flat),
-        lumped_mass.reshape(flat),
-        pixel_weights,
-        cut_element,
-        pixel_block,
-        jnp.asarray(radial_matrix()),
-        jnp.asarray(azimuth_table()),
-    )
+    )(*[pltpu.with_memory_space_constraint(x, pltpu.HBM) for x in operands])
+    advected, images = pl.pallas_call(
+        write_kernel,
+        out_shape=(
+            jax.ShapeDtypeStruct(flat, F32),
+            jax.ShapeDtypeStruct((2, NBLK, 128), F32),
+        ),
+        in_specs=[on_chip] * 3,
+        out_specs=(hbm, hbm),
+        scratch_shapes=[pltpu.VMEM((2, NBLK, 128), F32), dma((5,))],
+        compiler_params=pltpu.CompilerParams(vmem_limit_bytes=16 * 1024 * 1024),
+    )(*[pltpu.with_memory_space_constraint(x, pltpu.VMEM) for x in results])
     return advected.reshape(scalar.shape), images
 
 

time: 40.2 us -> 35.3 us (0.88)
  local copies, waits for them, and re-layouts: 4.57 us -> 0 us
    unnamed x2 -> x0, local copies, waits for them, and re-layouts: 4.57 us -> none
    pallas_call x1 -> x2, Pallas kernels: 34.8 us -> 34.6 us  [the longest x1 33 us: per_device(): pl.pallas_call(functools.partial(kernel, sizes), out_shape=outputs, in_sp...]
where the time goes in v3:
time: 35.3 us; the launch traced here: 35.2 us
  Pallas kernels  34.6 us (98%)
  between operations  0.64 us (2%)
    pallas_call x1, Pallas kernels, per_device(): pl.pallas_call(functools.partial(kernel, sizes), out_shape=outputs, in_sp...  33 us
    pallas_call x1, Pallas kernels, per_device(): pl.pallas_call(write_kernel, out_shape=(jax.ShapeDtypeStruct(flat, F32),...  1.55 us

profile of v3, /device:TPU:1, one launch (start us, length us, event | category | flops | bytes accessed | tf_op | source)
XLA Modules:
  0.0 35.2 jit_solution(1984997121232963287)
XLA Ops:
  0.6 33.0 %shard_map.95 = (f32[32,64,128]{2,1,0:T(8,128)S(1)}, bf16[4,2,128,128]{3,2,1,0:T(8,128)(2,1)S(1)}, bf16[2,1024,512]{2,1,0:T(8,128)(2,1)S(1)}) custom-call(f32[32,64,128]{2,1,0:T(8,128)} %bitcast.5, f32[3,32,64,128]{3,2,1,0:T(8,128)} %bitcast.4, f32[32,64,128]{2,1,0:T(8,128)} %bitcast.6, bf16[8,512,128]{2,1,0:T(8,128)(2,1)} %wts_h.1, s32[8,128]{1,0:T(8,128)} %cut_h.1, ...), custom_call_target="tpu_custom_call" | custom-call | tf_op jit(solution)/shard_map/pallas_call | solution.py:603
  33.6 1.5 %shard_map.96 = (f32[32,64,128]{2,1,0:T(8,128)}, f32[2,1024,128]{2,1,0:T(8,128)}) custom-call(f32[32,64,128]{2,1,0:T(8,128)S(1)} %get-tuple-element.7.adv, bf16[4,2,128,128]{3,2,1,0:T(8,128)(2,1)S(1)} %get-tuple-element.8.values, bf16[2,1024,512]{2,1,0:T(8,128)(2,1)S(1)} %get-tuple-element.9.img_hot), custom_call_target="tpu_custom_call" | custom-call | tf_op jit(solution)/shard_map/pallas_call | solution.py:643

commit v4 on v3

--- a/solution.py
+++ b/solution.py
@@ -67,6 +67,8 @@
     shifts = np.stack([DERIV[rows, (rows + d) % 8] for d in range(8)])
     return np.broadcast_to(shifts[:, :, None], (8, 8, 128)).astype(np.float32)
 
+
+AXIAL = (1, 2, 0, 3)
 
 SIGNS = [
     (sx, sy, sz)
@@ -146,9 +148,10 @@
     load_cut = load(cut_h, cut, in_sem.at[5])
     load_wts = load(wts_h, wts, in_sem.at[6])
 
+    peers = {s: peer(*s) for s in SIGNS}
     barrier = pltpu.get_barrier_semaphore()
-    for s in SIGNS:
-        pl.semaphore_signal(barrier, inc=1, device_id=peer(*s), device_id_type=pl.DeviceIdType.MESH)
+    for s in sorted(SIGNS, key=lambda s: -abs(s[0])):
+        pl.semaphore_signal(barrier, inc=1, device_id=peers[s], device_id_type=pl.DeviceIdType.MESH)
     for d in range(2, n_cam - 1):
         pl.semaphore_signal(
             barrier, inc=1, device_id=peer(0, 0, d), device_id_type=pl.DeviceIdType.MESH
@@ -161,9 +164,10 @@
     take_prev = (lane % 8 == 0) & (lane != 0)
     edge = (lane == 0) | (lane == 127)
     zero = jnp.zeros((8, 128), F32)
-    from_upper = jnp.where(cam < n_cam - 1, 1.0, 0.0).astype(F32)
-    from_lower = jnp.where(cam > 0, 1.0, 0.0).astype(F32)
-    keep = jnp.where(even, jnp.full((8, 128), from_upper), jnp.full((8, 128), from_lower))
+    has_upper, has_lower = cam < n_cam - 1, cam > 0
+    from_upper = jnp.where(has_upper, 1.0, 0.0).astype(F32)
+    from_lower = jnp.where(has_lower, 1.0, 0.0).astype(F32)
+    keep = jnp.where(even, jnp.full((8, 128), from_upper), jnp.full((8, 128), from_lower)) > 0.5
 
     def lane_pairs(g):
         return (
@@ -181,25 +185,49 @@
         return outer
 
     copies = []
-    waits = {}
-
-    def send(src, dst, e, group, s):
-        which = e * 26 + SIGNS.index(s)
+
+    def send(src, dst, e, group, slot, s):
         copy = pltpu.make_async_remote_copy(
             src_ref=src,
             dst_ref=dst,
-            send_sem=send_sem.at[which],
-            recv_sem=recv_sem.at[which],
-            device_id=peer(*s),
+            send_sem=send_sem.at[slot],
+            recv_sem=recv_sem.at[slot],
+            device_id=peers[s],
             device_id_type=pl.DeviceIdType.MESH,
         )
-        copy.start()
-        copies.append(copy)
-        waits.setdefault((e, group), []).append(copy)
-
-    def wait_for(e, group):
-        for copy in waits[e, group]:
-            copy.wait_recv()
+        copies.append((e, group, s[2], copy))
+        if s[2] == 0:
+            copy.start()
+
+    def toward(sz, body):
+        pl.when(has_upper if sz > 0 else has_lower)(body)
+
+    def launch(sz, body):
+        first_new = len(copies)
+        body()
+        chosen = [copy for _, _, _, copy in copies[first_new:]]
+
+        def start():
+            for copy in chosen:
+                copy.start()
+
+        toward(sz, start)
+
+    def wait_all(e, groups, received):
+        for sz in (0, -1, 1):
+            chosen = [c for at, group, z, c in copies if at == e and group in groups and z == sz]
+
+            def body(chosen=chosen):
+                for copy in chosen:
+                    if received:
+                        copy.wait_recv()
+                    else:
+                        copy.wait_send()
+
+            if sz == 0:
+                body()
+            else:
+                toward(-sz if received else sz, body)
 
     def pair_azimuth(ref, a):
         for i in range(8):
@@ -221,42 +249,60 @@
             parts[at % 4] = jnp.where(here, pltpu.roll(piece, 2 * spot + 1, 1), parts[at % 4])
         return (parts[0] + parts[1]) + (parts[2] + parts[3])
 
-    def pack_ends(ref, e, kind):
+    def pair_plane(plane):
+        both = plane[pl.ds(7, 7, stride=8), :] + plane[pl.ds(8, 7, stride=8), :]
+        plane[pl.ds(7, 7, stride=8), :] = both
+        plane[pl.ds(8, 7, stride=8), :] = both
+
+    def pack_ends(e, kind):
         plane, tile = faces[e][0], faces[e][1]
         for px in (0, 1):
-            plane[px, kind] = ref[31 * px]
             tile[px, kind] = gather_columns(
-                [(56 * px + b, ref[31 * px, 8 * b : 8 * b + 8, :]) for b in range(8)]
+                [(56 * px + b, plane[px, kind, 8 * b : 8 * b + 8, :]) for b in range(8)]
             )
 
     def send_ends(e):
         plane, tile, _, _, _, r_plane, r_xy, r_xz, r_xyz, _, _, _ = faces[e]
+        base = 30 * e
         for px in (0, 1):
             sx = 2 * px - 1
-            send(plane.at[px], r_plane.at[px], e, "ends", (sx, 0, 0))
+            send(plane.at[px], r_plane.at[px], e, "ends", base + px, (sx, 0, 0))
             for py in (0, 1):
                 send(
                     plane.at[px, :, pl.ds(56 * py, 8)],
                     r_xy.at[px, py],
                     e,
                     "ends",
+                    base + 2 + 2 * px + py,
                     (sx, 2 * py - 1, 0),
                 )
-            for pz in (0, 1):
-                sz = 2 * pz - 1
-                send(tile.at[px], r_xz.at[px, pz], e, "ends", (sx, 0, sz))
-                for py in (0, 1):
-                    send(tile.at[px], r_xyz.at[px, py, pz], e, "ends", (sx, 2 * py - 1, sz))
-
-    def pack_rest(ref, e, kind):
-        rows, cols, lines = faces[e][2:5]
-        for n in range(32):
-            rows[0, kind, n : n + 1, :] = ref[n, 0:1, :]
-            rows[1, kind, n : n + 1, :] = ref[n, 63:64, :]
-
-        @pl.loop(0, 4)
-        def _(a):
-            cols[a, kind] = gather_columns(
+        for pz in (0, 1):
+            sz = 2 * pz - 1
+
+            def body(pz=pz, sz=sz):
+                for px in (0, 1):
+                    sx = 2 * px - 1
+                    slot = base + 6 + 6 * pz + 3 * px
+                    send(tile.at[px], r_xz.at[px, pz], e, "ends", slot, (sx, 0, sz))
+                    for py in (0, 1):
+                        send(
+                            tile.at[px],
+                            r_xyz.at[px, py, pz],
+                            e,
+                            "ends",
+                            slot + 1 + py,
+                            (sx, 2 * py - 1, sz),
+                        )
+
+            launch(sz, body)
+
+    def pack_columns(ref, e, kind, half):
+        cols = faces[e][3]
+
+        @pl.loop(0, 2)
+        def _(t):
+            a = 3 * t if half else 1 + t
+            cols[2 * half + t, kind] = gather_columns(
                 [
                     (8 * i + b, ref[8 * a + i, 8 * b : 8 * b + 8, :])
                     for i in range(8)
@@ -264,44 +310,95 @@
                 ]
             )
 
+    def send_columns(e, half):
+        cols, r_cols = faces[e][3], faces[e][10]
+        for pz in (0, 1):
+            sz = 2 * pz - 1
+
+            def body(pz=pz, sz=sz):
+                part = pl.ds(2 * half, 2)
+                send(
+                    cols.at[part],
+                    r_cols.at[pz, part],
+                    e,
+                    "rest",
+                    30 * e + 18 + 2 * pz + half,
+                    (0, 0, sz),
+                )
+
+            launch(sz, body)
+
+    def pack_lines(e, kind):
+        cols, lines = faces[e][3], faces[e][4]
         low, high = zero, zero
-        for a in range(4):
-            low = jnp.where(sub == a, jnp.broadcast_to(cols[a, kind, 0:1, :], (8, 128)), low)
-            high = jnp.where(sub == a, jnp.broadcast_to(cols[a, kind, 7:8, :], (8, 128)), high)
+        for at in range(4):
+            low = jnp.where(sub == at, jnp.broadcast_to(cols[at, kind, 0:1, :], (8, 128)), low)
+            high = jnp.where(sub == at, jnp.broadcast_to(cols[at, kind, 7:8, :], (8, 128)), high)
         lines[0, kind] = low
         lines[1, kind] = high
 
-    def send_rest(e):
-        rows, cols, lines = faces[e][2:5]
-        r_rows, r_cols, r_yz = faces[e][9:12]
+    def send_lines(e):
+        lines, r_yz = faces[e][4], faces[e][11]
         for pz in (0, 1):
             sz = 2 * pz - 1
-            send(cols, r_cols.at[pz], e, "rest", (0, 0, sz))
-            for py in (0, 1):
-                send(lines.at[py], r_yz.at[py, pz], e, "rest", (0, 2 * py - 1, sz))
+
+            def body(pz=pz, sz=sz):
+                for py in (0, 1):
+                    send(
+                        lines.at[py],
+                        r_yz.at[py, pz],
+                        e,
+                        "rest",
+                        30 * e + 22 + 2 * pz + py,
+                        (0, 2 * py - 1, sz),
+                    )
+
+            launch(sz, body)
+
+    def pack_rows(ref, e, kind):
+        rows = faces[e][2]
+        for n in range(32):
+            rows[0, kind, n : n + 1, :] = ref[n, 0:1, :]
+            rows[1, kind, n : n + 1, :] = ref[n, 63:64, :]
+
+    def send_rows(e):
+        rows, r_rows = faces[e][2], faces[e][9]
         for py in (0, 1):
-            send(rows.at[py], r_rows.at[py], e, "rest", (0, 2 * py - 1, 0))
+            send(rows.at[py], r_rows.at[py], e, "rest", 30 * e + 26 + py, (0, 2 * py - 1, 0))
 
     def across_azimuth(t, py):
         t = pltpu.roll(t, 114 if py else 14, 1)
         return jnp.where((lane % 16 < 2) if py else (lane % 16 >= 14), t, zero)
 
     def swap(q):
-        return jnp.where(even, pltpu.roll(q, 127, 1), pltpu.roll(q, 1, 1)) * keep
+        return jnp.where(keep, jnp.where(even, pltpu.roll(q, 127, 1), pltpu.roll(q, 1, 1)), zero)
 
     def add_rest(ref, e, kind):
         r_rows, r_cols, r_yz = faces[e][9:12]
         for n in range(32):
-            ref[n, 0:1, :] = ref[n, 0:1, :] + r_rows[1, kind, n : n + 1, :]
-            ref[n, 63:64, :] = ref[n, 63:64, :] + r_rows[0, kind, n : n + 1, :]
+            after, before = r_rows[1, kind, n : n + 1, :], r_rows[0, kind, n : n + 1, :]
+            if 0 < n < 31 and n % 8 in (0, 7):
+                other = n + 1 if n % 8 == 7 else n - 1
+                after = after + r_rows[1, kind, other : other + 1, :]
+                before = before + r_rows[0, kind, other : other + 1, :]
+            ref[n, 0:1, :] = ref[n, 0:1, :] + after
+            ref[n, 63:64, :] = ref[n, 63:64, :] + before
         across = [
             across_azimuth(jnp.where(even, r_yz[py, 1, kind], r_yz[py, 0, kind]), py)
             for py in (0, 1)
         ]
+        found = [None] * 4
+        for at, a in enumerate(AXIAL):
+            q = jnp.where(even, r_cols[1, at, kind], r_cols[0, at, kind])
+            q = q + jnp.where(sub == 0, jnp.broadcast_to(across[1][at : at + 1, :], (8, 128)), zero)
+            q = q + jnp.where(sub == 7, jnp.broadcast_to(across[0][at : at + 1, :], (8, 128)), zero)
+            found[a] = q
         for a in range(4):
-            q = jnp.where(even, r_cols[1, a, kind], r_cols[0, a, kind])
-            q = q + jnp.where(sub == 0, jnp.broadcast_to(across[1][a : a + 1, :], (8, 128)), zero)
-            q = q + jnp.where(sub == 7, jnp.broadcast_to(across[0][a : a + 1, :], (8, 128)), zero)
+            q = found[a]
+            if a < 3:
+                q = q + jnp.where(lane >= 112, pltpu.roll(found[a + 1], 112, 1), zero)
+            if a > 0:
+                q = q + jnp.where(lane < 16, pltpu.roll(found[a - 1], 16, 1), zero)
             xcol[kind, a] = swap(q)
 
     def add_ends(ref, e, kind):
@@ -331,14 +428,40 @@
             edge, pltpu.roll(x, 127 - 2 * spot, 1), zero
         )
 
-    def convect(src, a):
-        block = src[pl.ds(8 * a, 8)].reshape(512, 128)
+    def along_radius(block):
         high = block.astype(BF16)
         low = (block - high.astype(F32)).astype(BF16)
         both = jnp.dot(
             jnp.concatenate([high, low], axis=1), tab[...], preferred_element_type=F32
         )
-        radial[...] = (both[:, :128] + both[:, 128:]).reshape(8, 64, 128)
+        return both[:, :128] + both[:, 128:]
+
+    def along_azimuth(f):
+        turned = azi[0] * f
+        for d in range(1, 8):
+            turned = turned + azi[d] * pltpu.roll(f, 8 - d, 0)
+        return turned
+
+    def convect_plane(src, e, px):
+        n, i = 31 * px, 7 * px
+        plane = faces[e][0].at[px, 0]
+        turning = along_radius(src[n])
+        for b in range(8):
+            part = slice(8 * b, 8 * b + 8)
+            axial = None
+            for p in range(8):
+                term = float(DERIV[i, p]) * src[n - i + p, part, :]
+                axial = term if axial is None else axial + term
+            c = (
+                vel[0, n, part, :] * axial
+                + vel[1, n, part, :] * along_azimuth(src[n, part, :])
+                + vel[2, n, part, :] * turning[part, :]
+            )
+            plane[part, :] = lane_pairs(mass[n, part, :] * c)
+        pair_plane(plane)
+
+    def convect(src, a):
+        radial[...] = along_radius(src[pl.ds(8 * a, 8)].reshape(512, 128)).reshape(8, 64, 128)
         for b in range(8):
             part = slice(8 * b, 8 * b + 8)
             f = [src[8 * a + i, part, :] for i in range(8)]
@@ -356,16 +479,25 @@
                 axial[7 - i] = y - x
             for i in range(8):
                 n = 8 * a + i
-                turned = azi[0] * f[i]
-                for d in range(1, 8):
-                    turned = turned + azi[d] * pltpu.roll(f[i], 8 - d, 0)
                 c = (
                     vel[0, n, part, :] * axial[i]
-                    + vel[1, n, part, :] * turned
+                    + vel[1, n, part, :] * along_azimuth(f[i])
                     + vel[2, n, part, :] * radial[i, part, :]
                 )
                 g_ref[n, part, :] = lane_pairs(mass[n, part, :] * c)
         pair_azimuth(g_ref, a)
+
+    for pz in (0, 1):
+
+        @pl.when(jnp.logical_not(has_lower if pz else has_upper))
+        def _(pz=pz):
+            for _, _, _, _, _, _, _, r_xz, r_xyz, _, r_cols, r_yz in faces:
+                r_cols[pz] = jnp.zeros(r_cols.shape[1:], F32)
+                for px in (0, 1):
+                    r_xz[px, pz] = jnp.zeros(r_xz.shape[2:], F32)
+                    r_yz[px, pz] = jnp.zeros(r_yz.shape[2:], F32)
+                    for py in (0, 1):
+                        r_xyz[px, py, pz] = jnp.zeros(r_xyz.shape[3:], F32)
 
     load_mass.wait()
 
@@ -377,28 +509,47 @@
                 winv[n, part, :] = lane_pairs(mass[n, part, :])
         pair_azimuth(winv, a)
 
+    for px in (0, 1):
+        faces[0][0][px, 1] = winv[31 * px]
+    pack_ends(0, 1)
+    for half in (0, 1):
+        pack_columns(winv, 0, 1, half)
+    pack_lines(0, 1)
+    pack_rows(winv, 0, 1)
     pair_axial(winv)
-    pack_ends(winv, 0, 1)
-    pack_rest(winv, 0, 1)
 
     load_fld.wait()
     load_tab.wait()
     load_azi.wait()
 
+    def wait_velocity(a):
+        part = pl.ds(8 * a, 8)
+        pltpu.make_async_copy(vel_h.at[:, part], vel.at[:, part], vel_sem.at[a]).wait()
+
+    for px in (0, 1):
+        wait_velocity(3 * px)
+        convect_plane(fld, 0, px)
+    pack_ends(0, 0)
+    pl.semaphore_wait(barrier, 26 + n_cam - 3)
+    send_ends(0)
+    wait_velocity(1)
+    wait_velocity(2)
+
     @twice
     def stage_one(a):
-        part = pl.ds(pl.multiple_of(8 * a, 8), 8)
-        pltpu.make_async_copy(vel_h.at[:, part], vel.at[:, part], vel_sem.at[a]).wait()
         convect(fld, a)
 
+    stage_one("middle")
+    pack_columns(g_ref, 0, 0, 0)
+    send_columns(0, 0)
     stage_one("ends")
-    pack_ends(g_ref, 0, 0)
-    pl.semaphore_wait(barrier, 26 + n_cam - 3)
-    send_ends(0)
-    stage_one("middle")
+    pack_columns(g_ref, 0, 0, 1)
+    send_columns(0, 1)
+    pack_lines(0, 0)
+    send_lines(0)
+    pack_rows(g_ref, 0, 0)
+    send_rows(0)
     pair_axial(g_ref)
-    pack_rest(g_ref, 0, 0)
-    send_rest(0)
 
     load_blk.wait()
     blk_copies = []
@@ -425,12 +576,12 @@
         chosen = jnp.broadcast_to(cut[pl.ds(m, 1), :].astype(F32), (128, 128)).T
         place = lax.broadcasted_iota(jnp.int32, (128, 128), 1).astype(F32)
         for q in range(4):
-            cut_hot[m, :, 128 * q : 128 * q + 128] = jnp.where(
+            cut_hot[m // 2, pl.ds(128 * (m % 2), 128), 128 * q : 128 * q + 128] = jnp.where(
                 chosen == place + 128.0 * q, 1.0, 0.0
             ).astype(BF16)
 
     @twice
-    def stage_two(a):
+    def step_one(a):
         x, y = xcol[0, a], xcol[1, a]
         for i in range(8):
             for b in range(8):
@@ -438,21 +589,34 @@
                 factor = -STEP / total(winv, y, n, i, b)
                 winv[n, part, :] = factor
                 first[n, part, :] = fld[n, part, :] + factor * total(g_ref, x, n, i, b)
+
+    @twice
+    def stage_two(a):
         convect(first, a)
 
-    wait_for(0, "rest")
+    wait_all(0, ("rest",), True)
     add_rest(winv, 0, 1)
     add_rest(g_ref, 0, 0)
+    step_one("middle")
     stage_two("middle")
-    wait_for(0, "ends")
+    pack_columns(g_ref, 1, 0, 0)
+    send_columns(1, 0)
+    wait_all(0, ("ends",), True)
     add_ends(winv, 0, 1)
     add_ends(g_ref, 0, 0)
+    step_one("ends")
+    for px in (0, 1):
+        convect_plane(first, 1, px)
+    pack_ends(1, 0)
+    send_ends(1)
     stage_two("ends")
-    pack_ends(g_ref, 1, 0)
-    send_ends(1)
+    pack_columns(g_ref, 1, 0, 1)
+    send_columns(1, 1)
+    pack_lines(1, 0)
+    send_lines(1)
+    pack_rows(g_ref, 1, 0)
+    send_rows(1)
     pair_axial(g_ref)
-    pack_rest(g_ref, 1, 0)
-    send_rest(1)
 
     for copy in blk_copies:
         copy.wait_recv()
@@ -502,20 +666,21 @@
                         16 * h : 16 * h + 16, 128 * c : 128 * c + 128
                     ]
 
-    wait_for(1, "rest")
+    wait_all(1, ("rest",), True)
     add_rest(g_ref, 1, 0)
     finish("middle")
-    wait_for(1, "ends")
+    wait_all(1, ("ends",), True)
     add_ends(g_ref, 1, 0)
     finish("ends")
 
     v_copies = []
     for d in sorted(range(1, n_cam), key=lambda d: -min(d, n_cam - d)) + [0]:
         q = lax.rem(cam + d, n_cam)
+        picked = jnp.dot(cut_hot[q], elems[...], preferred_element_type=F32).astype(BF16)
         for t in range(2):
-            m = 2 * q + t
-            picked = jnp.dot(cut_hot[m], elems[...], preferred_element_type=F32).astype(BF16)
-            value = jnp.dot(picked, wts_p[m], preferred_element_type=F32).astype(BF16)
+            value = jnp.dot(
+                picked[128 * t : 128 * t + 128], wts_p[2 * q + t], preferred_element_type=F32
+            ).astype(BF16)
             if d:
                 v_send[d, t] = value
             else:
@@ -532,7 +697,9 @@
             copy.start()
             v_copies.append(copy)
 
-    for copy in copies + blk_copies:
+    for e in (0, 1):
+        wait_all(e, ("ends", "rest"), False)
+    for copy in blk_copies:
         copy.wait_send()
     for copy in v_copies:
         copy.wait_recv()
@@ -623,14 +790,14 @@
             pltpu.VMEM((2, 4, 8, 128), F32),
             pltpu.VMEM((512, 128), F32),
             pltpu.VMEM((8, 512, 128), BF16),
-            pltpu.VMEM((8, 128, 512), BF16),
+            pltpu.VMEM((4, 256, 512), BF16),
             pltpu.VMEM((512, 512), BF16),
             pltpu.VMEM((n_cam, 2, 128, 128), BF16),
             pltpu.VMEM((n_cam, 8, 128), jnp.int32),
             dma((7,)),
             dma((4,)),
-            dma((52,)),
-            dma((52,)),
+            dma((58,)),
+            dma((58,)),
             dma((n_cam,)),
             dma((n_cam,)),
             dma((n_cam,)),

time: 35.3 us -> 35 us (level)
  no operation moved by 1% of the time
where the time goes in v4:
time: 35 us; the launch traced here: 34.9 us
  Pallas kernels  34.3 us (98%)
  between operations  0.64 us (2%)
    pallas_call x1, Pallas kernels, per_device(): pl.pallas_call(functools.partial(kernel, sizes), out_shape=outputs, in_sp...  32.7 us
    pallas_call x1, Pallas kernels, per_device(): pl.pallas_call(write_kernel, out_shape=(jax.ShapeDtypeStruct(flat, F32),...  1.55 us

profile of v4, /device:TPU:1, one launch (start us, length us, event | category | flops | bytes accessed | tf_op | source)
XLA Modules:
  0.0 34.9 jit_solution(18270208665938501951)
XLA Ops:
  0.6 32.7 %shard_map.95 = (f32[32,64,128]{2,1,0:T(8,128)S(1)}, bf16[4,2,128,128]{3,2,1,0:T(8,128)(2,1)S(1)}, bf16[2,1024,512]{2,1,0:T(8,128)(2,1)S(1)}) custom-call(f32[32,64,128]{2,1,0:T(8,128)} %bitcast.5, f32[3,32,64,128]{3,2,1,0:T(8,128)} %bitcast.4, f32[32,64,128]{2,1,0:T(8,128)} %bitcast.6, bf16[8,512,128]{2,1,0:T(8,128)(2,1)} %wts_h.1, s32[8,128]{1,0:T(8,128)} %cut_h.1, ...), custom_call_target="tpu_custom_call" | custom-call | tf_op jit(solution)/shard_map/pallas_call | solution.py:770
  33.4 1.5 %shard_map.96 = (f32[32,64,128]{2,1,0:T(8,128)}, f32[2,1024,128]{2,1,0:T(8,128)}) custom-call(f32[32,64,128]{2,1,0:T(8,128)S(1)} %get-tuple-element.7.adv, bf16[4,2,128,128]{3,2,1,0:T(8,128)(2,1)S(1)} %get-tuple-element.8.values, bf16[2,1024,512]{2,1,0:T(8,128)(2,1)S(1)} %get-tuple-element.9.img_hot), custom_call_target="tpu_custom_call" | custom-call | tf_op jit(solution)/shard_map/pallas_call | solution.py:810

commit v5 on v4

--- a/solution.py
+++ b/solution.py
@@ -62,6 +62,14 @@
     return np.block([[high, low], [high, np.zeros_like(low)]])
 
 
+def cross_matrix():
+    table = np.concatenate([np.kron(np.eye(8), DERIV), np.kron(DERIV, np.eye(8))])
+    table = table.astype(np.float32)
+    high = table.astype(ml_dtypes.bfloat16)
+    low = (table - high.astype(np.float32)).astype(ml_dtypes.bfloat16)
+    return np.concatenate([high, high, low], axis=1)
+
+
 def azimuth_table():
     rows = np.arange(8)
     shifts = np.stack([DERIV[rows, (rows + d) % 8] for d in range(8)])
@@ -89,6 +97,7 @@
     blk_h,
     tab_h,
     azi_h,
+    cross_h,
     adv,
     v_recv,
     img_hot,
@@ -100,6 +109,7 @@
     blk,
     tab,
     azi,
+    cross,
     g_ref,
     first,
     winv,
@@ -126,12 +136,21 @@
     cam, ex, ey = lax.axis_index("cam"), lax.axis_index("ex"), lax.axis_index("ey")
     faces = (faces_one, faces_two)
 
-    def peer(sx, sy, sz):
+    def beside(at, size):
         return {
-            "cam": lax.rem(cam + (sz + n_cam), n_cam),
-            "ex": lax.rem(ex + (sx + n_ex), n_ex),
-            "ey": lax.rem(ey + (sy + n_ey), n_ey),
+            0: at,
+            1: jnp.where(at == size - 1, 0, at + 1),
+            -1: jnp.where(at == 0, size - 1, at - 1),
         }
+
+    cams, exs, eys = beside(cam, n_cam), beside(ex, n_ex), beside(ey, n_ey)
+    peers = {s: {"cam": cams[s[2]], "ex": exs[s[0]], "ey": eys[s[1]]} for s in SIGNS}
+
+    def camera_owner(d):
+        return jnp.where(cam + d >= n_cam, cam + d - n_cam, cam + d)
+
+    def along_cam(d):
+        return {"cam": camera_owner(d), "ex": ex, "ey": ey}
 
     def load(src, dst, sem):
         copy = pltpu.make_async_copy(src, dst, sem)
@@ -142,20 +161,25 @@
     load_fld = load(scalar_h, fld, in_sem.at[1])
     load_tab = load(tab_h, tab, in_sem.at[2])
     load_azi = load(azi_h, azi, in_sem.at[3])
-    for a in (0, 3, 1, 2):
+    load_cross = load(cross_h, cross, in_sem.at[7])
+
+    def load_vel(a):
         load(vel_h.at[:, pl.ds(8 * a, 8)], vel.at[:, pl.ds(8 * a, 8)], vel_sem.at[a])
+
+    load_vel(0)
+    load_vel(3)
+    barrier = pltpu.get_barrier_semaphore()
+    for s in sorted(SIGNS, key=lambda s: (-abs(s[0]), -abs(s[2]), -abs(s[1]))):
+        pl.semaphore_signal(barrier, inc=1, device_id=peers[s], device_id_type=pl.DeviceIdType.MESH)
+    for d in range(2, n_cam - 1):
+        pl.semaphore_signal(
+            barrier, inc=1, device_id=along_cam(d), device_id_type=pl.DeviceIdType.MESH
+        )
+    load_vel(1)
+    load_vel(2)
     load_blk = load(blk_h, blk, in_sem.at[4])
     load_cut = load(cut_h, cut, in_sem.at[5])
     load_wts = load(wts_h, wts, in_sem.at[6])
-
-    peers = {s: peer(*s) for s in SIGNS}
-    barrier = pltpu.get_barrier_semaphore()
-    for s in sorted(SIGNS, key=lambda s: -abs(s[0])):
-        pl.semaphore_signal(barrier, inc=1, device_id=peers[s], device_id_type=pl.DeviceIdType.MESH)
-    for d in range(2, n_cam - 1):
-        pl.semaphore_signal(
-            barrier, inc=1, device_id=peer(0, 0, d), device_id_type=pl.DeviceIdType.MESH
-        )
 
     lane = lax.broadcasted_iota(jnp.int32, (8, 128), 1)
     sub = lax.broadcasted_iota(jnp.int32, (8, 128), 0)
@@ -462,29 +486,27 @@
 
     def convect(src, a):
         radial[...] = along_radius(src[pl.ds(8 * a, 8)].reshape(512, 128)).reshape(8, 64, 128)
-        for b in range(8):
-            part = slice(8 * b, 8 * b + 8)
-            f = [src[8 * a + i, part, :] for i in range(8)]
-            plus = [f[p] + f[7 - p] for p in range(4)]
-            minus = [f[p] - f[7 - p] for p in range(4)]
-            axial = [None] * 8
-            for i in range(4):
-                x = y = None
-                for p in range(4):
-                    alpha = float((DERIV[i, p] + DERIV[i, 7 - p]) / 2)
-                    beta = float((DERIV[i, p] - DERIV[i, 7 - p]) / 2)
-                    x = alpha * plus[p] if x is None else x + alpha * plus[p]
-                    y = beta * minus[p] if y is None else y + beta * minus[p]
-                axial[i] = x + y
-                axial[7 - i] = y - x
-            for i in range(8):
-                n = 8 * a + i
-                c = (
-                    vel[0, n, part, :] * axial[i]
-                    + vel[1, n, part, :] * along_azimuth(f[i])
-                    + vel[2, n, part, :] * radial[i, part, :]
-                )
-                g_ref[n, part, :] = lane_pairs(mass[n, part, :] * c)
+        for b in range(0, 8, 2):
+            pieces = []
+            for d in (b, b + 1):
+                block = src[pl.ds(8 * a, 8), 8 * d : 8 * d + 8, :].reshape(64, 128)
+                high = block.astype(BF16)
+                low = (block - high.astype(F32)).astype(BF16)
+                pieces.append(jnp.concatenate([high, low, high], axis=0))
+            both = jnp.dot(
+                cross[...], jnp.concatenate(pieces, axis=1), preferred_element_type=F32
+            )
+            for d in (0, 1):
+                part = slice(8 * (b + d), 8 * (b + d) + 8)
+                lanes = slice(128 * d, 128 * d + 128)
+                for i in range(8):
+                    n = 8 * a + i
+                    c = (
+                        vel[0, n, part, :] * both[64 + 8 * i : 72 + 8 * i, lanes]
+                        + vel[1, n, part, :] * both[8 * i : 8 * i + 8, lanes]
+                        + vel[2, n, part, :] * radial[i, part, :]
+                    )
+                    g_ref[n, part, :] = lane_pairs(mass[n, part, :] * c)
         pair_azimuth(g_ref, a)
 
     for pz in (0, 1):
@@ -521,6 +543,7 @@
     load_fld.wait()
     load_tab.wait()
     load_azi.wait()
+    load_cross.wait()
 
     def wait_velocity(a):
         part = pl.ds(8 * a, 8)
@@ -559,7 +582,7 @@
             dst_ref=blk_recv.at[d],
             send_sem=b_send_sem.at[d],
             recv_sem=b_recv_sem.at[d],
-            device_id=peer(0, 0, d),
+            device_id=along_cam(d),
             device_id_type=pl.DeviceIdType.MESH,
         )
         copy.start()
@@ -586,7 +609,7 @@
         for i in range(8):
             for b in range(8):
                 n, part = 8 * a + i, slice(8 * b, 8 * b + 8)
-                factor = -STEP / total(winv, y, n, i, b)
+                factor = -STEP * pl.reciprocal(total(winv, y, n, i, b))
                 winv[n, part, :] = factor
                 first[n, part, :] = fld[n, part, :] + factor * total(g_ref, x, n, i, b)
 
@@ -594,21 +617,19 @@
     def stage_two(a):
         convect(first, a)
 
-    wait_all(0, ("rest",), True)
-    add_rest(winv, 0, 1)
-    add_rest(g_ref, 0, 0)
-    step_one("middle")
-    stage_two("middle")
-    pack_columns(g_ref, 1, 0, 0)
-    send_columns(1, 0)
-    wait_all(0, ("ends",), True)
-    add_ends(winv, 0, 1)
-    add_ends(g_ref, 0, 0)
+    wait_all(0, ("ends", "rest"), True)
+    for ref, kind in ((winv, 1), (g_ref, 0)):
+        add_rest(ref, 0, kind)
+        add_ends(ref, 0, kind)
     step_one("ends")
     for px in (0, 1):
         convect_plane(first, 1, px)
     pack_ends(1, 0)
     send_ends(1)
+    step_one("middle")
+    stage_two("middle")
+    pack_columns(g_ref, 1, 0, 0)
+    send_columns(1, 0)
     stage_two("ends")
     pack_columns(g_ref, 1, 0, 1)
     send_columns(1, 1)
@@ -675,7 +696,7 @@
 
     v_copies = []
     for d in sorted(range(1, n_cam), key=lambda d: -min(d, n_cam - d)) + [0]:
-        q = lax.rem(cam + d, n_cam)
+        q = camera_owner(d)
         picked = jnp.dot(cut_hot[q], elems[...], preferred_element_type=F32).astype(BF16)
         for t in range(2):
             value = jnp.dot(
@@ -691,7 +712,7 @@
                 dst_ref=v_recv.at[d],
                 send_sem=v_send_sem.at[d],
                 recv_sem=v_recv_sem.at[d],
-                device_id=peer(0, 0, d),
+                device_id=along_cam(d),
                 device_id_type=pl.DeviceIdType.MESH,
             )
             copy.start()
@@ -766,11 +787,12 @@
         pixel_block,
         jnp.asarray(radial_matrix()),
         jnp.asarray(azimuth_table()),
+        jnp.asarray(cross_matrix()),
     )
     results = pl.pallas_call(
         functools.partial(kernel, sizes),
         out_shape=outputs,
-        in_specs=[hbm] * 8,
+        in_specs=[hbm] * 9,
         out_specs=(on_chip,) * 3,
         scratch_shapes=[
             big,
@@ -781,6 +803,7 @@
             pltpu.VMEM((8, 128), jnp.int32),
             pltpu.VMEM((256, 256), BF16),
             pltpu.VMEM((8, 8, 128), F32),
+            pltpu.VMEM((128, 192), BF16),
             big,
             big,
             big,
@@ -794,7 +817,7 @@
             pltpu.VMEM((512, 512), BF16),
             pltpu.VMEM((n_cam, 2, 128, 128), BF16),
             pltpu.VMEM((n_cam, 8, 128), jnp.int32),
-            dma((7,)),
+            dma((8,)),
             dma((4,)),
             dma((58,)),
             dma((58,)),

time: 35 us -> 33.9 us (0.969)
  Pallas kernels: 34.3 us -> 33.2 us
    pallas_call x1, Pallas kernels: 32.7 us -> 31.6 us  [per_device(): pl.pallas_call(functools.partial(kernel, sizes), out_shape=outputs, in_sp...]
where the time goes in v5:
time: 33.9 us; the launch traced here: 33.8 us
  Pallas kernels  33.2 us (98%)
  between operations  0.64 us (2%)
    pallas_call x1, Pallas kernels, per_device(): pl.pallas_call(functools.partial(kernel, sizes), out_shape=outputs, in_sp...  31.6 us
    pallas_call x1, Pallas kernels, per_device(): pl.pallas_call(write_kernel, out_shape=(jax.ShapeDtypeStruct(flat, F32),...  1.55 us

profile of v5, /device:TPU:1, one launch (start us, length us, event | category | flops | bytes accessed | tf_op | source)
XLA Modules:
  0.0 33.8 jit_solution(13316111884861545828)
XLA Ops:
  0.6 31.6 %shard_map.104 = (f32[32,64,128]{2,1,0:T(8,128)S(1)}, bf16[4,2,128,128]{3,2,1,0:T(8,128)(2,1)S(1)}, bf16[2,1024,512]{2,1,0:T(8,128)(2,1)S(1)}) custom-call(f32[32,64,128]{2,1,0:T(8,128)} %bitcast.5, f32[3,32,64,128]{3,2,1,0:T(8,128)} %bitcast.4, f32[32,64,128]{2,1,0:T(8,128)} %bitcast.6, bf16[8,512,128]{2,1,0:T(8,128)(2,1)} %wts_h.1, s32[8,128]{1,0:T(8,128)} %cut_h.1, ...), custom_call_target="tpu_custom_call" | custom-call | tf_op jit(solution)/shard_map/pallas_call | solution.py:792
  32.2 1.5 %shard_map.105 = (f32[32,64,128]{2,1,0:T(8,128)}, f32[2,1024,128]{2,1,0:T(8,128)}) custom-call(f32[32,64,128]{2,1,0:T(8,128)S(1)} %get-tuple-element.7.adv, bf16[4,2,128,128]{3,2,1,0:T(8,128)(2,1)S(1)} %get-tuple-element.8.values, bf16[2,1024,512]{2,1,0:T(8,128)(2,1)S(1)} %get-tuple-element.9.img_hot), custom_call_target="tpu_custom_call" | custom-call | tf_op jit(solution)/shard_map/pallas_call | solution.py:833

commit v6 on v5

--- a/solution.py
+++ b/solution.py
@@ -204,7 +204,7 @@
         def outer(which):
             @pl.loop(0, 2)
             def _(t):
-                body(3 * t if which == "ends" else 1 + t)
+                body(*((3 * t, 2 + t) if which == "ends" else (1 + t, t)))
 
         return outer
 
@@ -320,19 +320,17 @@
 
             launch(sz, body)
 
-    def pack_columns(ref, e, kind, half):
-        cols = faces[e][3]
-
-        @pl.loop(0, 2)
-        def _(t):
-            a = 3 * t if half else 1 + t
-            cols[2 * half + t, kind] = gather_columns(
-                [
-                    (8 * i + b, ref[8 * a + i, 8 * b : 8 * b + 8, :])
-                    for i in range(8)
-                    for b in range(8)
-                ]
-            )
+    def pick(parts, spot, piece):
+        here = (lane == 2 * spot) | (lane == 2 * spot + 1)
+        parts[spot % 4] = jnp.where(here, pltpu.roll(piece, 2 * spot + 1, 1), parts[spot % 4])
+
+    def put_columns(parts, e, kind, slot):
+        q = (parts[0] + parts[1]) + (parts[2] + parts[3])
+        after = pltpu.roll(pltpu.roll(q, 126, 1), 7, 0)
+        before = pltpu.roll(pltpu.roll(q, 2, 1), 1, 0)
+        q = q + jnp.where((sub == 7) & (lane % 16 < 14), after, zero)
+        q = q + jnp.where((sub == 0) & (lane % 16 >= 2), before, zero)
+        faces[e][3][slot, kind] = q
 
     def send_columns(e, half):
         cols, r_cols = faces[e][3], faces[e][10]
@@ -484,7 +482,8 @@
             plane[part, :] = lane_pairs(mass[n, part, :] * c)
         pair_plane(plane)
 
-    def convect(src, a):
+    def convect(src, a, e, slot):
+        parts = [zero] * 4
         radial[...] = along_radius(src[pl.ds(8 * a, 8)].reshape(512, 128)).reshape(8, 64, 128)
         for b in range(0, 8, 2):
             pieces = []
@@ -506,7 +505,10 @@
                         + vel[1, n, part, :] * both[8 * i : 8 * i + 8, lanes]
                         + vel[2, n, part, :] * radial[i, part, :]
                     )
-                    g_ref[n, part, :] = lane_pairs(mass[n, part, :] * c)
+                    g = mass[n, part, :] * c
+                    pick(parts, 8 * i + b + d, g)
+                    g_ref[n, part, :] = lane_pairs(g)
+        put_columns(parts, e, 0, slot)
         pair_azimuth(g_ref, a)
 
     for pz in (0, 1):
@@ -523,19 +525,22 @@
 
     load_mass.wait()
 
-    @pl.loop(0, 4)
-    def _(a):
+    @twice
+    def sum_mass(a, slot):
+        parts = [zero] * 4
         for i in range(8):
             for b in range(8):
                 n, part = 8 * a + i, slice(8 * b, 8 * b + 8)
+                pick(parts, 8 * i + b, mass[n, part, :])
                 winv[n, part, :] = lane_pairs(mass[n, part, :])
+        put_columns(parts, 0, 1, slot)
         pair_azimuth(winv, a)
 
+    sum_mass("ends")
+    sum_mass("middle")
     for px in (0, 1):
         faces[0][0][px, 1] = winv[31 * px]
     pack_ends(0, 1)
-    for half in (0, 1):
-        pack_columns(winv, 0, 1, half)
     pack_lines(0, 1)
     pack_rows(winv, 0, 1)
     pair_axial(winv)
@@ -559,14 +564,12 @@
     wait_velocity(2)
 
     @twice
-    def stage_one(a):
-        convect(fld, a)
+    def stage_one(a, slot):
+        convect(fld, a, 0, slot)
 
     stage_one("middle")
-    pack_columns(g_ref, 0, 0, 0)
     send_columns(0, 0)
     stage_one("ends")
-    pack_columns(g_ref, 0, 0, 1)
     send_columns(0, 1)
     pack_lines(0, 0)
     send_lines(0)
@@ -604,7 +607,7 @@
             ).astype(BF16)
 
     @twice
-    def step_one(a):
+    def step_one(a, _):
         x, y = xcol[0, a], xcol[1, a]
         for i in range(8):
             for b in range(8):
@@ -614,8 +617,8 @@
                 first[n, part, :] = fld[n, part, :] + factor * total(g_ref, x, n, i, b)
 
     @twice
-    def stage_two(a):
-        convect(first, a)
+    def stage_two(a, slot):
+        convect(first, a, 1, slot)
 
     wait_all(0, ("ends", "rest"), True)
     for ref, kind in ((winv, 1), (g_ref, 0)):
@@ -628,10 +631,8 @@
     send_ends(1)
     step_one("middle")
     stage_two("middle")
-    pack_columns(g_ref, 1, 0, 0)
     send_columns(1, 0)
     stage_two("ends")
-    pack_columns(g_ref, 1, 0, 1)
     send_columns(1, 1)
     pack_lines(1, 0)
     send_lines(1)
@@ -661,7 +662,7 @@
     ).astype(BF16)
 
     @twice
-    def finish(a):
+    def finish(a, _):
         x = xcol[0, a]
         for i in range(8):
             for b in range(8):

time: 33.9 us -> 33.6 us (level)
  no operation moved by 1% of the time
where the time goes in v6:
time: 33.6 us; the launch traced here: 33.5 us
  Pallas kernels  32.9 us (98%)
  between operations  0.64 us (2%)
    pallas_call x1, Pallas kernels, per_device(): pl.pallas_call(functools.partial(kernel, sizes), out_shape=outputs, in_sp...  31.3 us
    pallas_call x1, Pallas kernels, per_device(): pl.pallas_call(write_kernel, out_shape=(jax.ShapeDtypeStruct(flat, F32),...  1.55 us

profile of v6, /device:TPU:1, one launch (start us, length us, event | category | flops | bytes accessed | tf_op | source)
XLA Modules:
  0.0 33.5 jit_solution(919325700623366174)
XLA Ops:
  0.6 31.3 %shard_map.104 = (f32[32,64,128]{2,1,0:T(8,128)S(1)}, bf16[4,2,128,128]{3,2,1,0:T(8,128)(2,1)S(1)}, bf16[2,1024,512]{2,1,0:T(8,128)(2,1)S(1)}) custom-call(f32[32,64,128]{2,1,0:T(8,128)} %bitcast.5, f32[3,32,64,128]{3,2,1,0:T(8,128)} %bitcast.4, f32[32,64,128]{2,1,0:T(8,128)} %bitcast.6, bf16[8,512,128]{2,1,0:T(8,128)(2,1)} %wts_h.1, s32[8,128]{1,0:T(8,128)} %cut_h.1, ...), custom_call_target="tpu_custom_call" | custom-call | tf_op jit(solution)/shard_map/pallas_call | solution.py:793
  31.9 1.5 %shard_map.105 = (f32[32,64,128]{2,1,0:T(8,128)}, f32[2,1024,128]{2,1,0:T(8,128)}) custom-call(f32[32,64,128]{2,1,0:T(8,128)S(1)} %get-tuple-element.7.adv, bf16[4,2,128,128]{3,2,1,0:T(8,128)(2,1)S(1)} %get-tuple-element.8.values, bf16[2,1024,512]{2,1,0:T(8,128)(2,1)S(1)} %get-tuple-element.9.img_hot), custom_call_target="tpu_custom_call" | custom-call | tf_op jit(solution)/shard_map/pallas_call | solution.py:834

commit v7 on v6

--- a/solution.py
+++ b/solution.py
@@ -103,6 +103,7 @@
     img_hot,
     fld,
     vel,
+    side,
     mass,
     wts,
     cut,
@@ -166,8 +167,9 @@
     def load_vel(a):
         load(vel_h.at[:, pl.ds(8 * a, 8)], vel.at[:, pl.ds(8 * a, 8)], vel_sem.at[a])
 
-    load_vel(0)
-    load_vel(3)
+    load_sides = [
+        load(vel_h.at[:, pl.ds(31 * px, 1)], side.at[px], vel_sem.at[4 + px]) for px in (0, 1)
+    ]
     barrier = pltpu.get_barrier_semaphore()
     for s in sorted(SIGNS, key=lambda s: (-abs(s[0]), -abs(s[2]), -abs(s[1]))):
         pl.semaphore_signal(barrier, inc=1, device_id=peers[s], device_id_type=pl.DeviceIdType.MESH)
@@ -175,11 +177,8 @@
         pl.semaphore_signal(
             barrier, inc=1, device_id=along_cam(d), device_id_type=pl.DeviceIdType.MESH
         )
-    load_vel(1)
-    load_vel(2)
     load_blk = load(blk_h, blk, in_sem.at[4])
     load_cut = load(cut_h, cut, in_sem.at[5])
-    load_wts = load(wts_h, wts, in_sem.at[6])
 
     lane = lax.broadcasted_iota(jnp.int32, (8, 128), 1)
     sub = lax.broadcasted_iota(jnp.int32, (8, 128), 0)
@@ -475,9 +474,9 @@
                 term = float(DERIV[i, p]) * src[n - i + p, part, :]
                 axial = term if axial is None else axial + term
             c = (
-                vel[0, n, part, :] * axial
-                + vel[1, n, part, :] * along_azimuth(src[n, part, :])
-                + vel[2, n, part, :] * turning[part, :]
+                side[px, 0, 0, part, :] * axial
+                + side[px, 1, 0, part, :] * along_azimuth(src[n, part, :])
+                + side[px, 2, 0, part, :] * turning[part, :]
             )
             plane[part, :] = lane_pairs(mass[n, part, :] * c)
         pair_plane(plane)
@@ -524,6 +523,9 @@
                         r_xyz[px, py, pz] = jnp.zeros(r_xyz.shape[3:], F32)
 
     load_mass.wait()
+    for a in (1, 2, 0, 3):
+        load_vel(a)
+    load_wts = load(wts_h, wts, in_sem.at[6])
 
     @twice
     def sum_mass(a, slot):
@@ -555,13 +557,13 @@
         pltpu.make_async_copy(vel_h.at[:, part], vel.at[:, part], vel_sem.at[a]).wait()
 
     for px in (0, 1):
-        wait_velocity(3 * px)
+        load_sides[px].wait()
         convect_plane(fld, 0, px)
     pack_ends(0, 0)
     pl.semaphore_wait(barrier, 26 + n_cam - 3)
     send_ends(0)
-    wait_velocity(1)
-    wait_velocity(2)
+    for a in range(4):
+        wait_velocity(a)
 
     @twice
     def stage_one(a, slot):
@@ -798,6 +800,7 @@
         scratch_shapes=[
             big,
             pltpu.VMEM((3,) + flat, F32),
+            pltpu.VMEM((2, 3, 1, 64, 128), F32),
             big,
             pltpu.VMEM((8, 512, 128), BF16),
             pltpu.VMEM((8, 128), jnp.int32),
@@ -819,7 +822,7 @@
             pltpu.VMEM((n_cam, 2, 128, 128), BF16),
             pltpu.VMEM((n_cam, 8, 128), jnp.int32),
             dma((8,)),
-            dma((4,)),
+            dma((6,)),
             dma((58,)),
             dma((58,)),
             dma((n_cam,)),

time: 33.6 us -> 33.7 us (level)
  no operation moved by 1% of the time
where the time goes in v7:
time: 33.7 us; the launch traced here: 33.5 us
  Pallas kernels  32.9 us (98%)
  between operations  0.64 us (2%)
    pallas_call x1, Pallas kernels, per_device(): pl.pallas_call(functools.partial(kernel, sizes), out_shape=outputs, in_sp...  31.3 us
    pallas_call x1, Pallas kernels, per_device(): pl.pallas_call(write_kernel, out_shape=(jax.ShapeDtypeStruct(flat, F32),...  1.55 us

profile of v7, /device:TPU:1, one launch (start us, length us, event | category | flops | bytes accessed | tf_op | source)
XLA Modules:
  0.0 33.5 jit_solution(11118558913262442486)
XLA Ops:
  0.6 31.3 %shard_map.104 = (f32[32,64,128]{2,1,0:T(8,128)S(1)}, bf16[4,2,128,128]{3,2,1,0:T(8,128)(2,1)S(1)}, bf16[2,1024,512]{2,1,0:T(8,128)(2,1)S(1)}) custom-call(f32[32,64,128]{2,1,0:T(8,128)} %bitcast.5, f32[3,32,64,128]{3,2,1,0:T(8,128)} %bitcast.4, f32[32,64,128]{2,1,0:T(8,128)} %bitcast.6, bf16[8,512,128]{2,1,0:T(8,128)(2,1)} %wts_h.1, s32[8,128]{1,0:T(8,128)} %cut_h.1, ...), custom_call_target="tpu_custom_call" | custom-call | tf_op jit(solution)/shard_map/pallas_call | solution.py:795
  32.0 1.5 %shard_map.105 = (f32[32,64,128]{2,1,0:T(8,128)}, f32[2,1024,128]{2,1,0:T(8,128)}) custom-call(f32[32,64,128]{2,1,0:T(8,128)S(1)} %get-tuple-element.7.adv, bf16[4,2,128,128]{3,2,1,0:T(8,128)(2,1)S(1)} %get-tuple-element.8.values, bf16[2,1024,512]{2,1,0:T(8,128)(2,1)S(1)} %get-tuple-element.9.img_hot), custom_call_target="tpu_custom_call" | custom-call | tf_op jit(solution)/shard_map/pallas_call | solution.py:837

commit v8 on v7

--- a/solution.py
+++ b/solution.py
@@ -285,7 +285,7 @@
             )
 
     def send_ends(e):
-        plane, tile, _, _, _, r_plane, r_xy, r_xz, r_xyz, _, _, _ = faces[e]
+        plane, r_plane, r_xy = faces[e][0], faces[e][5], faces[e][6]
         base = 30 * e
         for px in (0, 1):
             sx = 2 * px - 1
@@ -299,6 +299,10 @@
                     base + 2 + 2 * px + py,
                     (sx, 2 * py - 1, 0),
                 )
+
+    def send_end_columns(e):
+        tile, r_xz, r_xyz = faces[e][1], faces[e][7], faces[e][8]
+        base = 30 * e
         for pz in (0, 1):
             sz = 2 * pz - 1
 
@@ -559,9 +563,10 @@
     for px in (0, 1):
         load_sides[px].wait()
         convect_plane(fld, 0, px)
-    pack_ends(0, 0)
     pl.semaphore_wait(barrier, 26 + n_cam - 3)
     send_ends(0)
+    pack_ends(0, 0)
+    send_end_columns(0)
     for a in range(4):
         wait_velocity(a)
 
@@ -629,8 +634,9 @@
     step_one("ends")
     for px in (0, 1):
         convect_plane(first, 1, px)
+    send_ends(1)
     pack_ends(1, 0)
-    send_ends(1)
+    send_end_columns(1)
     step_one("middle")
     stage_two("middle")
     send_columns(1, 0)

time: 33.7 us -> 33.7 us (level)
  no operation moved by 1% of the time
where the time goes in v8:
time: 33.7 us; the launch traced here: 33.5 us
  Pallas kernels  32.9 us (98%)
  between operations  0.64 us (2%)
    pallas_call x1, Pallas kernels, per_device(): pl.pallas_call(functools.partial(kernel, sizes), out_shape=outputs, in_sp...  31.3 us
    pallas_call x1, Pallas kernels, per_device(): pl.pallas_call(write_kernel, out_shape=(jax.ShapeDtypeStruct(flat, F32),...  1.55 us

profile of v8, /device:TPU:1, one launch (start us, length us, event | category | flops | bytes accessed | tf_op | source)
XLA Modules:
  0.0 33.5 jit_solution(7992788321880648335)
XLA Ops:
  0.6 31.3 %shard_map.104 = (f32[32,64,128]{2,1,0:T(8,128)S(1)}, bf16[4,2,128,128]{3,2,1,0:T(8,128)(2,1)S(1)}, bf16[2,1024,512]{2,1,0:T(8,128)(2,1)S(1)}) custom-call(f32[32,64,128]{2,1,0:T(8,128)} %bitcast.5, f32[3,32,64,128]{3,2,1,0:T(8,128)} %bitcast.4, f32[32,64,128]{2,1,0:T(8,128)} %bitcast.6, bf16[8,512,128]{2,1,0:T(8,128)(2,1)} %wts_h.1, s32[8,128]{1,0:T(8,128)} %cut_h.1, ...), custom_call_target="tpu_custom_call" | custom-call | tf_op jit(solution)/shard_map/pallas_call | solution.py:801
  32.0 1.5 %shard_map.105 = (f32[32,64,128]{2,1,0:T(8,128)}, f32[2,1024,128]{2,1,0:T(8,128)}) custom-call(f32[32,64,128]{2,1,0:T(8,128)S(1)} %get-tuple-element.7.adv, bf16[4,2,128,128]{3,2,1,0:T(8,128)(2,1)S(1)} %get-tuple-element.8.values, bf16[2,1024,512]{2,1,0:T(8,128)(2,1)S(1)} %get-tuple-element.9.img_hot), custom_call_target="tpu_custom_call" | custom-call | tf_op jit(solution)/shard_map/pallas_call | solution.py:843
